TPU v7x, 128 devices: a whole 4x4x4 slice. The times are simulated.
128 devices in a mesh: dp: 32 (over z, y, core), tm: 4 (over x).
Axes of the slice: x: 4, y: 4, z: 4, core: 2. Of those that a mesh axis runs over, the one named last changes fastest.
Arguments:
- student: bfloat16 [256, 1024, 128], P(('dp', 'tm')), may hold values from -6 to 6
- teacher: bfloat16 [256, 1024, 128], P(('dp', 'tm')), may hold values from -200 to 200
- partner_dp: int32 [256, 8], replicated, may hold values from 0 to 31, all different within a row; in each aligned block of 2 rows (0 to 1, 2 to 3, ...) no two rows name the same one
- partner_slot: int32 [256, 8], replicated, may hold values from 0 to 1
- valid_frames: int32 [256], replicated, may hold values from 256 to 1024, as said below
Outputs:
- loss: float32 [], replicated
- grad_student: bfloat16 [256, 1024, 128], P(('dp', 'tm'))
Inputs may be any that keep to these rules, and one draw needn't show every extreme that they name: `partner_dp`: among the partner entries of the 2 blocks of one device no dp index appears more than 1 times; the 8 entries of one block are distinct. A partner may be the block itself. `valid_frames`: block 0 is full and block 1 has the fewest valid frames.
All inputs are finite; a program needn't handle non-finite values.
Results may differ from a plain program's by a relative error of at most 0.0042.
Values may be sent and summed in bfloat16 or wider, within the bound.
A program may use at most 64 MiB of HBM per device.

v0:
```python
import math

import jax
import jax.numpy as jnp
from jax import lax
from jax.sharding import PartitionSpec as P

NEG_FILL = -1e30


def body(student, teacher, partner_dp, partner_slot, valid_frames):
    peer_count = lax.axis_size("dp")
    time_count = lax.axis_size("tm")
    my_dp = lax.axis_index("dp")
    my_tm = lax.axis_index("tm")
    local_blocks, frames, proj_width = student.shape
    partner_count = partner_dp.shape[1]
    entries = local_blocks * partner_count
    slot_depth = (entries + peer_count - 1) // peer_count
    slot_total = peer_count * slot_depth
    score_scale = 1.0 / math.sqrt(proj_width)
    dest_all = lax.dynamic_index_in_dim(
        partner_dp.reshape(peer_count, time_count, entries), my_tm, 1, keepdims=False
    )
    source_all = lax.dynamic_index_in_dim(
        partner_slot.reshape(peer_count, time_count, entries), my_tm, 1, keepdims=False
    )
    earlier = jnp.tril(jnp.ones((entries, entries), jnp.int32), -1)
    same_dest = (dest_all[:, :, None] == dest_all[:, None, :]).astype(jnp.int32)
    rank_all = jnp.sum(same_dest * earlier[None], axis=2)
    my_dest = lax.dynamic_index_in_dim(dest_all, my_dp, 0, keepdims=False)
    my_source = lax.dynamic_index_in_dim(source_all, my_dp, 0, keepdims=False)
    my_rank = lax.dynamic_index_in_dim(rank_all, my_dp, 0, keepdims=False)
    entry_slot = my_dest * slot_depth + my_rank
    depth_ids = jnp.arange(slot_depth, dtype=jnp.int32)
    wanted = (dest_all == my_dp)[:, :, None] & (rank_all[:, :, None] == depth_ids[None, None, :])
    in_use = jnp.any(wanted, axis=1).reshape(slot_total)
    local_block = jnp.sum(jnp.where(wanted, source_all[:, :, None], 0), axis=1).reshape(slot_total)
    block_base = (my_dp * time_count + my_tm) * local_blocks
    frame_ids = jnp.arange(frames, dtype=jnp.int32)
    own_len = lax.dynamic_slice_in_dim(valid_frames, block_base, local_blocks)
    far_len = valid_frames[(my_dest * time_count + my_tm) * local_blocks + my_source]
    query_ok = frame_ids[None, :] < own_len[:, None]
    everyone = lax.all_gather(teacher, "dp", axis=0, tiled=True)
    far_keys = everyone[my_dest * local_blocks + my_source]
    keys_all = jnp.concatenate(
        [teacher[:, None], far_keys.reshape(local_blocks, partner_count, frames, proj_width)],
        axis=1,
    )
    lens_all = jnp.concatenate(
        [own_len[:, None], far_len.reshape(local_blocks, partner_count)], axis=1
    )
    keys_tiled = jnp.swapaxes(keys_all, 0, 1)
    lens_tiled = jnp.swapaxes(lens_all, 0, 1)

    def first_pass(inputs):
        key_block, lengths = inputs
        scores = (
            jnp.einsum("aie,aje->aij", student, key_block, preferred_element_type=jnp.float32)
            * score_scale
        )
        key_ok = frame_ids[None, :] < lengths[:, None]
        row_masked = jnp.where(key_ok[:, None, :], scores, NEG_FILL)
        row_best = jnp.max(row_masked, axis=2)
        row_sum = jnp.sum(jnp.exp(row_masked - row_best[:, :, None]), axis=2)
        col_masked = jnp.where(query_ok[:, :, None], scores, NEG_FILL)
        col_best = jnp.max(col_masked, axis=1)
        col_sum = jnp.sum(jnp.exp(col_masked - col_best[:, None, :]), axis=1)
        return (row_best, row_sum, col_best, col_sum)

    row_best, row_sum, col_best, col_sum = lax.map(first_pass, (keys_tiled, lens_tiled))
    row_top = jnp.max(row_best, axis=0)
    row_lse = row_top + jnp.log(jnp.sum(row_sum * jnp.exp(row_best - row_top[None]), axis=0))
    far_best = jnp.swapaxes(col_best[1:], 0, 1).reshape(entries, frames)
    far_sum = jnp.swapaxes(col_sum[1:], 0, 1).reshape(entries, frames)
    back_best = jnp.full((slot_total, frames), NEG_FILL, jnp.float32).at[entry_slot].set(far_best)
    back_sum = jnp.zeros((slot_total, frames), jnp.float32).at[entry_slot].set(far_sum)
    inc_best, inc_sum = (
        lax.all_to_all(back_best, "dp", split_axis=0, concat_axis=0, tiled=True),
        lax.all_to_all(back_sum, "dp", split_axis=0, concat_axis=0, tiled=True),
    )
    chosen = (local_block[:, None] == jnp.arange(local_blocks, dtype=jnp.int32)[None, :]) & in_use[
        :, None
    ]
    cand_best = jnp.where(chosen[:, :, None], inc_best[:, None, :], NEG_FILL)
    merged_best = jnp.maximum(col_best[0], jnp.max(cand_best, axis=0))
    merged_sum = col_sum[0] * jnp.exp(col_best[0] - merged_best)
    merged_sum = merged_sum + jnp.sum(
        jnp.where(
            chosen[:, :, None], inc_sum[:, None, :] * jnp.exp(cand_best - merged_best[None]), 0.0
        ),
        axis=0,
    )
    col_lse = merged_best + jnp.log(jnp.where(query_ok, merged_sum, 1.0))
    lse_out = jnp.where(in_use[:, None], col_lse[local_block], 0.0)
    lse_in = lax.all_to_all(lse_out, "dp", split_axis=0, concat_axis=0, tiled=True)
    far_lse = lse_in[entry_slot].reshape(local_blocks, partner_count, frames)
    lse_tiled = jnp.swapaxes(jnp.concatenate([col_lse[:, None], far_lse], axis=1), 0, 1)
    positive = (
        jnp.sum(student.astype(jnp.float32) * teacher.astype(jnp.float32), axis=2) * score_scale
    )
    row_terms = jnp.sum(jnp.where(query_ok, row_lse - positive, 0.0))
    col_terms = jnp.sum(jnp.where(query_ok, col_lse - positive, 0.0))
    loss_sum = lax.psum(0.5 * (row_terms + col_terms), ("dp", "tm"))
    loss = loss_sum / jnp.sum(valid_frames).astype(jnp.float32)
    diagonal = frame_ids[:, None] == frame_ids[None, :]

    def second_pass(inputs):
        key_block, lengths, key_lse, tile_index = inputs
        scores = (
            jnp.einsum("aie,aje->aij", student, key_block, preferred_element_type=jnp.float32)
            * score_scale
        )
        key_ok = frame_ids[None, :] < lengths[:, None]
        pair_ok = query_ok[:, :, None] & key_ok[:, None, :]
        prob_row = jnp.exp(scores - row_lse[:, :, None])
        prob_col = jnp.exp(scores - key_lse[:, None, :])
        grad_scores = jnp.where(pair_ok, 0.5 * (prob_row + prob_col), 0.0)
        grad_scores = grad_scores - jnp.where(
            (tile_index == 0) & diagonal[None] & query_ok[:, :, None], 1.0, 0.0
        )
        return jnp.einsum(
            "aij,aje->aie",
            grad_scores.astype(jnp.bfloat16),
            key_block,
            preferred_element_type=jnp.float32,
        )

    tile_ids = jnp.arange(partner_count + 1, dtype=jnp.int32)
    pieces = lax.map(second_pass, (keys_tiled, lens_tiled, lse_tiled, tile_ids))
    grad_student = (jnp.sum(pieces, axis=0) * score_scale).astype(jnp.bfloat16)
    return (loss, grad_student)


def solution(mesh):
    placed = (P(("dp", "tm"), None, None), P(("dp", "tm"), None, None), P(), P(), P())
    return jax.shard_map(
        body,
        mesh=mesh,
        in_specs=placed,
        out_specs=(P(), P(("dp", "tm"), None, None)),
        check_vma=False,
    )
```

profile of v0, /device:TPU:7, one launch (start us, length us, event | category | flops | bytes accessed | tf_op | source)
XLA Modules:
  0.0 383.4 jit_solution(9657005875069770102)
XLA Ops:
  15.3 70.4 %all-gather.2.cloned.1.call-done = bf16[64,1024,128]{2,1,0:T(8,128)(2,1)} async-done(((bf16[2,1024,128]{2,1,0:T(8,128)(2,1)}), bf16[64,1024,128]{2,1,0:T(8,128)(2,1)}) %all-gather.2.cloned.1.call-update) | async-done | bytes 16777232 | tf_op jit(solution)/shard_map/all_gather | solution.py:44
  85.7 8.8 %gather_fusion.1 = bf16[16,1024,128]{2,1,0:T(8,128)(2,1)} fusion(bf16[64,1024,128]{2,1,0:T(8,128)(2,1)} %all-gather.2.cloned.1.call-done, s32[1024]{0:T(1024)S(1)} %pad_clamp_fusion.2), kind=kCustom, calls=%fused_computation.1 | custom fusion | bytes 8388672 | tf_op jit(solution)/shard_map/gather | solution.py:45
  99.8 74.8 %while.28 = (s32[]{:T(128)}, f32[9,2,1024]{2,1,0:T(2,128)S(1)}, f32[9,2,1024]{2,1,0:T(2,128)S(1)}, f32[9,2,1024]{2,1,0:T(2,128)S(1)}, f32[9,2,1024]{2,1,0:T(2,12...) while((s32[]{:T(128)}, f32[9,2,1024]{2,1,0:T(2,128)S(1)}, ...), condition=%wide.region_5.6_spmd.clone, body=%wide.region_0.5_spmd.clone.sunk | while | flops 562032640 | bytes 17952924 | solution.py:71
  103.4 4.6 %fusion.84 = (f32[2,1024]{1,0:T(2,128)S(1)}, f32[2,1024]{1,0:T(2,128)S(1)}) fusion(f32[2,1024,1024]{2,1,0:T(8,128)S(1)} %get-tuple-element.479, f32[2,1024]{1,0:T(2,128)S(1)} %get-tuple-element.480, pred[2,1024]{1,0:T(4,128)(4,1)S(1)} %iota_compare_fusion.10, f32[2,1024]{1,0:T(2,128)S(1)} %get-tuple-element.481, ...), kind=kLoop, calls=%fused_computation.14.clone.1 | loop fusion | flops 14675968 | bytes 8425472 | tf_op jit(solution)/shard_map/while/body/eval_jaxpr/reduce_sum | solution.py:68
  111.7 4.6 %fusion.84 = (f32[2,1024]{1,0:T(2,128)S(1)}, f32[2,1024]{1,0:T(2,128)S(1)}) fusion(f32[2,1024,1024]{2,1,0:T(8,128)S(1)} %get-tuple-element.479, f32[2,1024]{1,0:T(2,128)S(1)} %get-tuple-element.480, pred[2,1024]{1,0:T(4,128)(4,1)S(1)} %iota_compare_fusion.10, f32[2,1024]{1,0:T(2,128)S(1)} %get-tuple-element.481, ...), kind=kLoop, calls=%fused_computation.14.clone.1 | loop fusion | flops 14675968 | bytes 8425472 | tf_op jit(solution)/shard_map/while/body/eval_jaxpr/reduce_sum | solution.py:68
  116.6 3.5 bitcast_reduce_fusion.3
  120.0 4.6 %fusion.84 = (f32[2,1024]{1,0:T(2,128)S(1)}, f32[2,1024]{1,0:T(2,128)S(1)}) fusion(f32[2,1024,1024]{2,1,0:T(8,128)S(1)} %get-tuple-element.479, f32[2,1024]{1,0:T(2,128)S(1)} %get-tuple-element.480, pred[2,1024]{1,0:T(4,128)(4,1)S(1)} %iota_compare_fusion.10, f32[2,1024]{1,0:T(2,128)S(1)} %get-tuple-element.481, ...), kind=kLoop, calls=%fused_computation.14.clone.1 | loop fusion | flops 14675968 | bytes 8425472 | tf_op jit(solution)/shard_map/while/body/eval_jaxpr/reduce_sum | solution.py:68
  128.3 4.6 %fusion.84 = (f32[2,1024]{1,0:T(2,128)S(1)}, f32[2,1024]{1,0:T(2,128)S(1)}) fusion(f32[2,1024,1024]{2,1,0:T(8,128)S(1)} %get-tuple-element.479, f32[2,1024]{1,0:T(2,128)S(1)} %get-tuple-element.480, pred[2,1024]{1,0:T(4,128)(4,1)S(1)} %iota_compare_fusion.10, f32[2,1024]{1,0:T(2,128)S(1)} %get-tuple-element.481, ...), kind=kLoop, calls=%fused_computation.14.clone.1 | loop fusion | flops 14675968 | bytes 8425472 | tf_op jit(solution)/shard_map/while/body/eval_jaxpr/reduce_sum | solution.py:68
  136.7 4.6 %fusion.84 = (f32[2,1024]{1,0:T(2,128)S(1)}, f32[2,1024]{1,0:T(2,128)S(1)}) fusion(f32[2,1024,1024]{2,1,0:T(8,128)S(1)} %get-tuple-element.479, f32[2,1024]{1,0:T(2,128)S(1)} %get-tuple-element.480, pred[2,1024]{1,0:T(4,128)(4,1)S(1)} %iota_compare_fusion.10, f32[2,1024]{1,0:T(2,128)S(1)} %get-tuple-element.481, ...), kind=kLoop, calls=%fused_computation.14.clone.1 | loop fusion | flops 14675968 | bytes 8425472 | tf_op jit(solution)/shard_map/while/body/eval_jaxpr/reduce_sum | solution.py:68
  141.5 3.5 bitcast_reduce_fusion.3
  145.0 4.6 %fusion.84 = (f32[2,1024]{1,0:T(2,128)S(1)}, f32[2,1024]{1,0:T(2,128)S(1)}) fusion(f32[2,1024,1024]{2,1,0:T(8,128)S(1)} %get-tuple-element.479, f32[2,1024]{1,0:T(2,128)S(1)} %get-tuple-element.480, pred[2,1024]{1,0:T(4,128)(4,1)S(1)} %iota_compare_fusion.10, f32[2,1024]{1,0:T(2,128)S(1)} %get-tuple-element.481, ...), kind=kLoop, calls=%fused_computation.14.clone.1 | loop fusion | flops 14675968 | bytes 8425472 | tf_op jit(solution)/shard_map/while/body/eval_jaxpr/reduce_sum | solution.py:68
  153.3 4.6 %fusion.84 = (f32[2,1024]{1,0:T(2,128)S(1)}, f32[2,1024]{1,0:T(2,128)S(1)}) fusion(f32[2,1024,1024]{2,1,0:T(8,128)S(1)} %get-tuple-element.479, f32[2,1024]{1,0:T(2,128)S(1)} %get-tuple-element.480, pred[2,1024]{1,0:T(4,128)(4,1)S(1)} %iota_compare_fusion.10, f32[2,1024]{1,0:T(2,128)S(1)} %get-tuple-element.481, ...), kind=kLoop, calls=%fused_computation.14.clone.1 | loop fusion | flops 14675968 | bytes 8425472 | tf_op jit(solution)/shard_map/while/body/eval_jaxpr/reduce_sum | solution.py:68
  161.6 4.6 %fusion.84 = (f32[2,1024]{1,0:T(2,128)S(1)}, f32[2,1024]{1,0:T(2,128)S(1)}) fusion(f32[2,1024,1024]{2,1,0:T(8,128)S(1)} %get-tuple-element.479, f32[2,1024]{1,0:T(2,128)S(1)} %get-tuple-element.480, pred[2,1024]{1,0:T(4,128)(4,1)S(1)} %iota_compare_fusion.10, f32[2,1024]{1,0:T(2,128)S(1)} %get-tuple-element.481, ...), kind=kLoop, calls=%fused_computation.14.clone.1 | loop fusion | flops 14675968 | bytes 8425472 | tf_op jit(solution)/shard_map/while/body/eval_jaxpr/reduce_sum | solution.py:68
  169.9 4.6 %fusion.84 = (f32[2,1024]{1,0:T(2,128)S(1)}, f32[2,1024]{1,0:T(2,128)S(1)}) fusion(f32[2,1024,1024]{2,1,0:T(8,128)S(1)} %get-tuple-element.479, f32[2,1024]{1,0:T(2,128)S(1)} %get-tuple-element.480, pred[2,1024]{1,0:T(4,128)(4,1)S(1)} %iota_compare_fusion.10, f32[2,1024]{1,0:T(2,128)S(1)} %get-tuple-element.481, ...), kind=kLoop, calls=%fused_computation.14.clone.1 | loop fusion | flops 14675968 | bytes 8425472 | tf_op jit(solution)/shard_map/while/body/eval_jaxpr/reduce_sum | solution.py:68
  176.1 5.4 %all-to-all-start = ((f32[32,1,1024]{2,1,0:T(1,128)}), f32[32,1,1024]{2,1,0:T(1,128)S(1)}, u32[]{:S(2)}, u32[]{:S(2)}) async-start(f32[32,1,1024]{2,1,0:T(1,128)} %all_to_all.18), calls=%async_computation | async-start | bytes 262144 | tf_op jit(solution)/shard_map/all_to_all | solution.py:79
  183.8 5.3 %all-to-all-done = f32[32,1,1024]{2,1,0:T(1,128)S(1)} async-done(((f32[32,1,1024]{2,1,0:T(1,128)}), f32[32,1,1024]{2,1,0:T(1,128)S(1)}, u32[]{:S(2)}, u32[]{:S(2)}) %all-to-all-start) | async-done | bytes 131104 | tf_op jit(solution)/shard_map/all_to_all | solution.py:79
  189.1 3.9 %all-to-all-start.1 = ((f32[32,1,1024]{2,1,0:T(1,128)}), f32[32,1,1024]{2,1,0:T(1,128)S(1)}, u32[]{:S(2)}, u32[]{:S(2)}) async-start(f32[32,1,1024]{2,1,0:T(1,128)} %all_to_all.20), calls=%async_computation.1 | async-start | bytes 262144 | tf_op jit(solution)/shard_map/all_to_all | solution.py:80
  193.2 7.6 %all-to-all-done.1 = f32[32,1,1024]{2,1,0:T(1,128)S(1)} async-done(((f32[32,1,1024]{2,1,0:T(1,128)}), f32[32,1,1024]{2,1,0:T(1,128)S(1)}, u32[]{:S(2)}, u32[]{:S(2)}) %all-to-all-start.1) | async-done | bytes 131104 | tf_op jit(solution)/shard_map/all_to_all | solution.py:80
  203.6 62.7 %psum.7 = f32[]{:T(128)} all-reduce(f32[]{:T(128)S(6)} %mul.113), channel_id=1, replica_groups=mesh['dp'=32,'tm'=4] {'dp','tm'}, use_global_device_ids=true, to_apply=%region_18.19 | all-reduce | flops 1 | bytes 8 | tf_op jit(solution)/shard_map/psum | solution.py:104
  267.7 4.4 %all-to-all-start.2 = ((f32[32,1,1024]{2,1,0:T(1,128)}), f32[32,1,1024]{2,1,0:T(1,128)S(1)}, u32[]{:S(2)}, u32[]{:S(2)}) async-start(f32[32,1,1024]{2,1,0:T(1,128)} %copy.101), calls=%async_computation.2 | async-start | bytes 262144 | tf_op jit(solution)/shard_map/all_to_all | solution.py:96
  272.9 6.9 %all-to-all-done.2 = f32[32,1,1024]{2,1,0:T(1,128)S(1)} async-done(((f32[32,1,1024]{2,1,0:T(1,128)}), f32[32,1,1024]{2,1,0:T(1,128)S(1)}, u32[]{:S(2)}, u32[]{:S(2)}) %all-to-all-start.2) | async-done | bytes 131104 | tf_op jit(solution)/shard_map/all_to_all | solution.py:96
  280.4 89.9 %while.29 = (s32[]{:T(128)}, f32[9,2,1024,128]{3,2,1,0:T(8,128)}, s32[9,2]{1,0:T(8,128)S(1)}, bf16[9,2,1024,128]{3,2,1,0:T(8,128)(2,1)}, bf16[2,1024,128]{2,1,0:...) while((s32[]{:T(128)}, f32[9,2,1024,128]{3,2,1,0:T(8,128)}, ...), condition=%wide.region_21.22_spmd.clone, body=%wide.region_20.21_spmd.clone.sunk | while | flops 1098911744 | bytes 4761267 | solution.py:130
  282.1 8.3 %fusion.91 = f32[9,2,1024,128]{3,2,1,0:T(8,128)} fusion(f32[9,2,1024,128]{3,2,1,0:T(8,128)} %get-tuple-element.541, s32[]{:T(128)S(6)} %copy.138, f32[2,1024]{1,0:T(2,128)S(1)} %dynamic-slice_bitcast_fusion.3, f32[2,1024]{1,0:T(2,128)S(1)} %get-tuple-element.556, pred[1024,1024]{0,1:T(8,128)(4,1)S(1)} %fusion.89, ...), kind=kOutput, calls=%fused_computation.39.clone.1 | convolution fusion | flops 1096810496 | bytes 3692032 | tf_op jit(solution)/shard_map/while/body/eval_jaxpr/aij,aje->aie/dot_general | solution.py:122
  292.1 8.3 %fusion.91 = f32[9,2,1024,128]{3,2,1,0:T(8,128)} fusion(f32[9,2,1024,128]{3,2,1,0:T(8,128)} %get-tuple-element.541, s32[]{:T(128)S(6)} %copy.138, f32[2,1024]{1,0:T(2,128)S(1)} %dynamic-slice_bitcast_fusion.3, f32[2,1024]{1,0:T(2,128)S(1)} %get-tuple-element.556, pred[1024,1024]{0,1:T(8,128)(4,1)S(1)} %fusion.89, ...), kind=kOutput, calls=%fused_computation.39.clone.1 | convolution fusion | flops 1096810496 | bytes 3692032 | tf_op jit(solution)/shard_map/while/body/eval_jaxpr/aij,aje->aie/dot_general | solution.py:122
  302.1 8.3 %fusion.91 = f32[9,2,1024,128]{3,2,1,0:T(8,128)} fusion(f32[9,2,1024,128]{3,2,1,0:T(8,128)} %get-tuple-element.541, s32[]{:T(128)S(6)} %copy.138, f32[2,1024]{1,0:T(2,128)S(1)} %dynamic-slice_bitcast_fusion.3, f32[2,1024]{1,0:T(2,128)S(1)} %get-tuple-element.556, pred[1024,1024]{0,1:T(8,128)(4,1)S(1)} %fusion.89, ...), kind=kOutput, calls=%fused_computation.39.clone.1 | convolution fusion | flops 1096810496 | bytes 3692032 | tf_op jit(solution)/shard_map/while/body/eval_jaxpr/aij,aje->aie/dot_general | solution.py:122
  312.1 8.3 %fusion.91 = f32[9,2,1024,128]{3,2,1,0:T(8,128)} fusion(f32[9,2,1024,128]{3,2,1,0:T(8,128)} %get-tuple-element.541, s32[]{:T(128)S(6)} %copy.138, f32[2,1024]{1,0:T(2,128)S(1)} %dynamic-slice_bitcast_fusion.3, f32[2,1024]{1,0:T(2,128)S(1)} %get-tuple-element.556, pred[1024,1024]{0,1:T(8,128)(4,1)S(1)} %fusion.89, ...), kind=kOutput, calls=%fused_computation.39.clone.1 | convolution fusion | flops 1096810496 | bytes 3692032 | tf_op jit(solution)/shard_map/while/body/eval_jaxpr/aij,aje->aie/dot_general | solution.py:122
  322.0 8.3 %fusion.91 = f32[9,2,1024,128]{3,2,1,0:T(8,128)} fusion(f32[9,2,1024,128]{3,2,1,0:T(8,128)} %get-tuple-element.541, s32[]{:T(128)S(6)} %copy.138, f32[2,1024]{1,0:T(2,128)S(1)} %dynamic-slice_bitcast_fusion.3, f32[2,1024]{1,0:T(2,128)S(1)} %get-tuple-element.556, pred[1024,1024]{0,1:T(8,128)(4,1)S(1)} %fusion.89, ...), kind=kOutput, calls=%fused_computation.39.clone.1 | convolution fusion | flops 1096810496 | bytes 3692032 | tf_op jit(solution)/shard_map/while/body/eval_jaxpr/aij,aje->aie/dot_general | solution.py:122
  332.0 8.3 %fusion.91 = f32[9,2,1024,128]{3,2,1,0:T(8,128)} fusion(f32[9,2,1024,128]{3,2,1,0:T(8,128)} %get-tuple-element.541, s32[]{:T(128)S(6)} %copy.138, f32[2,1024]{1,0:T(2,128)S(1)} %dynamic-slice_bitcast_fusion.3, f32[2,1024]{1,0:T(2,128)S(1)} %get-tuple-element.556, pred[1024,1024]{0,1:T(8,128)(4,1)S(1)} %fusion.89, ...), kind=kOutput, calls=%fused_computation.39.clone.1 | convolution fusion | flops 1096810496 | bytes 3692032 | tf_op jit(solution)/shard_map/while/body/eval_jaxpr/aij,aje->aie/dot_general | solution.py:122
  341.9 8.3 %fusion.91 = f32[9,2,1024,128]{3,2,1,0:T(8,128)} fusion(f32[9,2,1024,128]{3,2,1,0:T(8,128)} %get-tuple-element.541, s32[]{:T(128)S(6)} %copy.138, f32[2,1024]{1,0:T(2,128)S(1)} %dynamic-slice_bitcast_fusion.3, f32[2,1024]{1,0:T(2,128)S(1)} %get-tuple-element.556, pred[1024,1024]{0,1:T(8,128)(4,1)S(1)} %fusion.89, ...), kind=kOutput, calls=%fused_computation.39.clone.1 | convolution fusion | flops 1096810496 | bytes 3692032 | tf_op jit(solution)/shard_map/while/body/eval_jaxpr/aij,aje->aie/dot_general | solution.py:122
  351.9 8.3 %fusion.91 = f32[9,2,1024,128]{3,2,1,0:T(8,128)} fusion(f32[9,2,1024,128]{3,2,1,0:T(8,128)} %get-tuple-element.541, s32[]{:T(128)S(6)} %copy.138, f32[2,1024]{1,0:T(2,128)S(1)} %dynamic-slice_bitcast_fusion.3, f32[2,1024]{1,0:T(2,128)S(1)} %get-tuple-element.556, pred[1024,1024]{0,1:T(8,128)(4,1)S(1)} %fusion.89, ...), kind=kOutput, calls=%fused_computation.39.clone.1 | convolution fusion | flops 1096810496 | bytes 3692032 | tf_op jit(solution)/shard_map/while/body/eval_jaxpr/aij,aje->aie/dot_general | solution.py:122
  361.9 8.4 %fusion.91 = f32[9,2,1024,128]{3,2,1,0:T(8,128)} fusion(f32[9,2,1024,128]{3,2,1,0:T(8,128)} %get-tuple-element.541, s32[]{:T(128)S(6)} %copy.138, f32[2,1024]{1,0:T(2,128)S(1)} %dynamic-slice_bitcast_fusion.3, f32[2,1024]{1,0:T(2,128)S(1)} %get-tuple-element.556, pred[1024,1024]{0,1:T(8,128)(4,1)S(1)} %fusion.89, ...), kind=kOutput, calls=%fused_computation.39.clone.1 | convolution fusion | flops 1096810496 | bytes 3692032 | tf_op jit(solution)/shard_map/while/body/eval_jaxpr/aij,aje->aie/dot_general | solution.py:122
  370.3 4.2 %reduce_sum.113 = f32[2,1024,128]{2,1,0:T(8,128)S(1)} reduce(f32[9,2,1024,128]{3,2,1,0:T(8,128)} %get-tuple-element.118, f32[]{:T(128)} %constant.134.clone.1), dimensions={0}, to_apply=%region_22.23 | reduce | flops 2097152 | bytes 10485764 | tf_op jit(solution)/shard_map/reduce_sum | solution.py:131
  (166 shorter events, 56.2 us)
Async XLA Ops:
  7.2 87.3 %copy-start.1 = (bf16[2,1024,128]{2,1,0:T(8,128)(2,1)S(1)}, bf16[2,1024,128]{2,1,0:T(8,128)(2,1)}, u32[]{:S(2)}) copy-start(bf16[2,1024,128]{2,1,0:T(8,128)(2,1)} %param.10) | copy-start | bytes 1572868
  7.2 78.5 %all-gather.2.cloned.1.call-start = ((), (), s32[]{:S(2)}) async-start(), calls=%async_computation.3 | async-start | bytes 17301504 | tf_op jit(solution)/shard_map/all_gather | solution.py:44
  94.5 5.3 %copy-start.2 = (bf16[2,1024,128]{2,1,0:T(8,128)(2,1)S(1)}, bf16[2,1024,128]{2,1,0:T(8,128)(2,1)}, u32[]{:S(2)}) copy-start(bf16[2,1024,128]{2,1,0:T(8,128)(2,1)} %param.9) | copy-start | bytes 1572868
  99.8 81.8 %copy-start = (s32[256]{0:T(256)S(1)}, s32[256]{0:T(256)}, u32[]{:S(2)}) copy-start(s32[256]{0:T(256)} %param.13) | copy-start | bytes 3076
  176.1 13.0 %all-to-all-start = ((f32[32,1,1024]{2,1,0:T(1,128)}), f32[32,1,1024]{2,1,0:T(1,128)S(1)}, u32[]{:S(2)}, u32[]{:S(2)}) async-start(f32[32,1,1024]{2,1,0:T(1,128)} %all_to_all.18), calls=%async_computation | async-start | bytes 262144 | tf_op jit(solution)/shard_map/all_to_all | solution.py:79
  189.1 11.6 %all-to-all-start.1 = ((f32[32,1,1024]{2,1,0:T(1,128)}), f32[32,1,1024]{2,1,0:T(1,128)S(1)}, u32[]{:S(2)}, u32[]{:S(2)}) async-start(f32[32,1,1024]{2,1,0:T(1,128)} %all_to_all.20), calls=%async_computation.1 | async-start | bytes 262144 | tf_op jit(solution)/shard_map/all_to_all | solution.py:80
  267.7 12.0 %all-to-all-start.2 = ((f32[32,1,1024]{2,1,0:T(1,128)}), f32[32,1,1024]{2,1,0:T(1,128)S(1)}, u32[]{:S(2)}, u32[]{:S(2)}) async-start(f32[32,1,1024]{2,1,0:T(1,128)} %copy.101), calls=%async_computation.2 | async-start | bytes 262144 | tf_op jit(solution)/shard_map/all_to_all | solution.py:96
Sparse Core Ops, SparseCore 0:
  10.2 75.3 all-gather.1
where the time goes:
time: 387 us; the launch traced here: 383 us
  matrix products  106 us (27%)
  waiting for transfers between devices  90.8 us (23%)
  blocking collectives  62.7 us (16%)
  other arithmetic  58.2 us (15%)
  local copies, waits for them, and re-layouts  27.6 us (7%)
  between operations  18.1 us (5%)
  starting transfers between devices  13.7 us (4%)
  loops' own time  6.51 us (2%)
    dot_general x9, matrix products, second_pass(): jnp.einsum('aij,aje->aie', grad_scores.astype(jnp.bfloat16), key_block, p...  74.6 us
    all_gather x1, waiting for transfers between devices, body(): everyone = lax.all_gather(teacher, 'dp', axis=0, tiled=True)  70.4 us
    psum x1, blocking collectives, body(): loss_sum = lax.psum(0.5 * (row_terms + col_terms), ('dp', 'tm'))  62.7 us
    reduce_sum x9, other arithmetic, first_pass(): col_sum = jnp.sum(jnp.exp(col_masked - col_best[:, None, :]), axis=1)  41.5 us
    dot_general x9, matrix products, first_pass(): jnp.einsum('aie,aje->aij', student, key_block, preferred_element_type=jnp...  31.2 us
    gather x1, local copies, waits for them, and re-layouts, body(): far_keys = everyone[my_dest * local_blocks + my_source]  8.78 us
  transfers between devices with their start and end apart: 4, of which 4 were waited for; matrix products, arithmetic and copies ran while one was open for 2% of the time, Pallas kernels for 0%

commit v1 on v0

v1 whole, which is shorter than its diff:
```python
import functools
import heapq
import math

import jax
import jax.numpy as jnp
from jax import lax
from jax.experimental import pallas as pl
from jax.experimental.pallas import tpu as pltpu
from jax.sharding import PartitionSpec as P

MESH = pl.DeviceIdType.MESH
F32 = jnp.float32
BIG = 1e30

ZP, ZM, YP, YM = range(4)
MOVE = {ZP: (1, 0), ZM: (-1, 0), YP: (0, 1), YM: (0, -1)}


PARTS = 2


def onward(tile, oz, oy, part):
    half = part * 2 // PARTS
    first, second = (oz, oy) if tile == 0 else (oy, oz)
    plus1, minus1 = (ZP, ZM) if tile == 0 else (YP, YM)
    plus2, minus2 = (YP, YM) if tile == 0 else (ZP, ZM)
    links = []
    if second == 0:
        if first == 0:
            links += [plus1, minus1]
        elif first == 1 and half == 0:
            links += [plus1]
        elif first == 3 and half == 1:
            links += [minus1]
        links += [plus2, minus2]
    elif second == 1 and half == 0:
        links += [plus2]
    elif second == 3 and half == 1:
        links += [minus2]
    return links


def moved(oz, oy, link):
    dz, dy = MOVE[link]
    return (oz + dz) % 4, (oy + dy) % 4


def plan():
    free = [0.0] * 4
    events, order, count = [], [], 0

    def send(unit, link, now):
        nonlocal count
        tile, oz, oy, half = unit
        start = max(now, free[link])
        free[link] = start + 1.0
        noz, noy = moved(oz, oy, link)
        heapq.heappush(events, (free[link] + 0.5, count, (tile, noz, noy, half), link))
        count += 1

    first = []
    for link in range(4):
        near = 0 if link in (ZP, ZM) else 1
        lead = 0 if link in (ZP, YP) else 1
        for tile in (near, 1 - near):
            for part in range(PARTS):
                first.append(((tile, 0, 0, part if lead == 0 else PARTS - 1 - part), link))
    first = [first[k * 2 * PARTS + i] for i in range(2 * PARTS) for k in range(4)]
    for unit, link in first:
        send(unit, link, 0.0)
    while events:
        now, _, unit, _ = heapq.heappop(events)
        out = onward(*unit)
        order.append((unit, out))
        for link in out:
            send(unit, link, now)
    return first, order, max(free)


def gather_kernel(rows, t_ref, out_ref, send_sem, recv_sem, peer_send, peer_recv, own_sem):
    half_rows = rows // PARTS
    me, tm = lax.axis_index("dp"), lax.axis_index("tm")
    z, y, c = me // 8, (me // 2) % 4, me % 2

    def dp_of(zz, yy, cc):
        return (zz * 4 + yy) * 2 + cc

    near = [
        dp_of((z + 1) % 4, y, c), dp_of((z + 3) % 4, y, c),
        dp_of(z, (y + 1) % 4, c), dp_of(z, (y + 3) % 4, c),
    ]
    peer = dp_of(z, y, 1 - c)
    barrier = pltpu.get_barrier_semaphore()
    for other in near + [peer]:
        pl.semaphore_signal(barrier, inc=1, device_id=(other, tm), device_id_type=MESH)
    pl.semaphore_wait(barrier, 5)

    first, order, _ = plan()
    sends = []

    def recv_id(unit):
        tile, oz, oy, half = unit
        return ((tile * 4 + oz) * 4 + oy) * PARTS + half

    def slot(unit):
        _, oz, oy, _ = unit
        return dp_of((z + 4 - oz) % 4, (y + 4 - oy) % 4, c)

    def place(ref, unit):
        tile, oz, oy, half = unit
        return ref.at[slot(unit), tile, pl.ds(half * half_rows, half_rows)]

    def source(unit):
        tile, oz, oy, half = unit
        if oz == 0 and oy == 0:
            return t_ref.at[tile, pl.ds(half * half_rows, half_rows)]
        return place(out_ref, unit)

    def send(unit, link):
        tile, oz, oy, half = unit
        copy = pltpu.make_async_remote_copy(
            src_ref=source(unit), dst_ref=place(out_ref, unit),
            send_sem=send_sem.at[len(sends)], recv_sem=recv_sem.at[recv_id((tile, *moved(oz, oy, link), half))],
            device_id=(near[link], tm), device_id_type=MESH,
        )
        copy.start()
        sends.append(copy)

    shares = []

    def share(unit):
        copy = pltpu.make_async_remote_copy(
            src_ref=source(unit), dst_ref=place(out_ref, unit),
            send_sem=peer_send.at[recv_id(unit)], recv_sem=peer_recv.at[recv_id(unit)],
            device_id=(peer, tm), device_id_type=MESH,
        )
        copy.start()
        shares.append(copy)

    for unit, link in first:
        send(unit, link)
    for tile in (0, 1):
        for half in range(PARTS):
            share((tile, 0, 0, half))
    own = pltpu.make_async_copy(t_ref, out_ref.at[me], own_sem)
    own.start()
    for unit, out in order:
        here = place(out_ref, unit)
        pltpu.make_async_remote_copy(
            src_ref=here, dst_ref=here, send_sem=send_sem.at[0], recv_sem=recv_sem.at[recv_id(unit)],
            device_id=(near[0], tm), device_id_type=MESH,
        ).wait_recv()
        for link in out:
            send(unit, link)
        share(unit)
    for copy in shares:
        copy.wait_send()
        copy.wait_recv()
    for copy in sends:
        copy.wait_send()
    own.wait()


def gather(teacher, dp=32):
    blocks, rows, width = teacher.shape
    first, order, _ = plan()
    n_sends = len(first) + sum(len(o) for _, o in order)
    return pl.pallas_call(
        functools.partial(gather_kernel, rows),
        out_shape=jax.ShapeDtypeStruct((dp, blocks, rows, width), teacher.dtype),
        in_specs=[pl.BlockSpec(memory_space=pltpu.VMEM)],
        out_specs=pl.BlockSpec(memory_space=pl.ANY),
        scratch_shapes=[
            pltpu.SemaphoreType.DMA((n_sends,)), pltpu.SemaphoreType.DMA((32 * PARTS,)),
            pltpu.SemaphoreType.DMA((32 * PARTS,)), pltpu.SemaphoreType.DMA((32 * PARTS,)), pltpu.SemaphoreType.DMA,
        ],
        compiler_params=pltpu.CompilerParams(collective_id=0, has_side_effects=True),
        name="gather",
    )(teacher)


LOW, HIGH = 2.0 ** -60, 2.0 ** 100
STEP = 256


def augment(ref, index, count, key):
    rows, width = ref.shape[-2], 128
    row = lax.broadcasted_iota(jnp.int32, (rows, width), 0)
    lane = lax.broadcasted_iota(jnp.int32, (rows, width), 1)
    mask = jnp.where(row < count, 0.0, -BIG)
    mine, other = (0, 1) if key else (1, 0)
    ref[index, :, width:] = jnp.where(lane == mine, mask, jnp.where(lane == other, 1.0, 0.0)).astype(ref.dtype)


def nt(a, b):
    return lax.dot_general(a, b, (((1,), (1,)), ((), ())), preferred_element_type=F32)


def fetch(meta, every, t_buf, sems, e):
    return pltpu.make_async_copy(every.at[meta[e]], t_buf.at[e, :, pl.ds(0, 128)], sems.at[e])


def first_kernel(tiles, step, meta, s_ref, every, row_ref, send_ref, own_ref, ok_ref, sum_ref,
                 t_buf, s_buf, acc, col, sems):
    frames, width = s_ref.shape[1], s_ref.shape[2]
    total = 2 * tiles
    c2 = 1.0 / math.sqrt(width) / math.log(2.0)
    scale = 1.0 / math.sqrt(width)
    for e in range(total):
        fetch(meta, every, t_buf, sems, e).start()
    for a in range(2):
        s_buf[a, :, :width] = s_ref[a]
        augment(s_buf, a, meta[3 * total + a], False)
    acc[...] = jnp.zeros_like(acc)
    ok_ref[0] = 1
    sum_ref[...] = jnp.zeros_like(sum_ref)
    lane = lax.broadcasted_iota(jnp.int32, (1, frames), 1)
    send_ref[...] = jnp.zeros_like(send_ref)

    def put(e, values):
        a, k = e // tiles, e % tiles

        @pl.when(k == 0)
        def _():
            for r in range(8):
                own_ref[a, r:r + 1, :] = values[:, r * 128:(r + 1) * 128]

        @pl.when(k != 0)
        def _():
            for r in range(8):
                send_ref[meta[2 * total + e], r:r + 1, :] = values[:, r * 128:(r + 1) * 128]

    def tile(e, carry):
        a = e // tiles
        keys = meta[total + e]
        fetch(meta, every, t_buf, sems, e).wait()
        augment(t_buf, e, keys, True)
        col[...] = jnp.zeros_like(col)
        chunks = (meta[3 * total + a] + step - 1) // step
        spans = (keys + STEP - 1) // STEP
        for v in range(1, frames // STEP + 1):
            @pl.when(spans == v)
            def _():
                def chunk(i, c):
                    rows = pl.ds(pl.multiple_of(i * step, step), step)
                    lhs = s_buf[a, rows, :]
                    part = acc[a, rows, :]
                    for j in range(v):
                        cols = slice(j * STEP, (j + 1) * STEP)
                        p = jnp.exp2(nt(lhs, t_buf[e, cols, :]) * c2)
                        for u in range(STEP // 128):
                            part = part + p[:, u * 128:(u + 1) * 128]
                        col[:, cols] += jnp.sum(p.reshape(step // 8, 8, STEP), axis=0)
                    acc[a, rows, :] = part
                    return c
                lax.fori_loop(0, chunks, chunk, 0)
        sums = jnp.sum(col[...], axis=0, keepdims=True)
        real = lane < keys
        low = jnp.min(jnp.where(real, sums, 1.0))
        high = jnp.max(jnp.where(real, sums, 1.0))

        @pl.when(jnp.logical_not((low >= LOW) & (high <= HIGH)))
        def _():
            ok_ref[0] = 0
        put(e, jnp.where(real, jnp.log(jnp.where(real, sums, 1.0)), -BIG))
        return carry

    lax.fori_loop(0, total, tile, 0)

    for a in range(2):
        count = meta[3 * total + a]
        row = lax.broadcasted_iota(jnp.int32, (frames, 128), 0)
        sums = jnp.broadcast_to(jnp.sum(acc[a], axis=1, keepdims=True), (frames, 128))
        sums = jnp.where(row < count, sums, 1.0)

        @pl.when(jnp.logical_not((jnp.min(sums) >= LOW) & (jnp.max(sums) <= HIGH)))
        def _():
            ok_ref[0] = 0
        row_ref[a] = jnp.log(sums)

    @pl.when(ok_ref[0] == 0)
    def _():
        row_ref[...] = jnp.full(row_ref.shape, -BIG, F32)
        acc[...] = jnp.zeros_like(acc)
        half = 128

        def slow_tile(e, carry):
            a = e // tiles
            col[0:1, :] = jnp.full((1, frames), -BIG, F32)
            col[1:2, :] = jnp.zeros((1, frames), F32)

            def slow_chunk(i, c):
                rows = pl.ds(pl.multiple_of(i * half, half), half)
                lhs = s_buf[a, rows, :]
                for j in range(frames // half):
                    cols = slice(j * half, (j + 1) * half)
                    sc = nt(lhs, t_buf[e, cols, :]) * scale
                    old = row_ref[a, rows, :]
                    new = jnp.maximum(old, jnp.broadcast_to(jnp.max(sc, axis=1, keepdims=True), (half, 128)))
                    acc[a, rows, :] = acc[a, rows, :] * jnp.exp(old - new) + jnp.broadcast_to(
                        jnp.sum(jnp.where(sc > -0.01 * BIG, jnp.exp(sc - new[:, :1]), 0.0), axis=1, keepdims=True), (half, 128))
                    row_ref[a, rows, :] = new
                    cold = col[0:1, cols]
                    cnew = jnp.maximum(cold, jnp.max(sc, axis=0, keepdims=True))
                    col[1:2, cols] = col[1:2, cols] * jnp.exp(cold - cnew) + jnp.sum(
                        jnp.where(sc > -0.01 * BIG, jnp.exp(sc - cnew), 0.0), axis=0, keepdims=True)
                    col[0:1, cols] = cnew
                return c
            lax.fori_loop(0, frames // half, slow_chunk, 0)
            real = lane < meta[total + e]
            put(e, jnp.where(real, col[0:1, :] + jnp.log(jnp.where(real, col[1:2, :], 1.0)), -BIG))
            return carry
        lax.fori_loop(0, total, slow_tile, 0)
        for a in range(2):
            row = lax.broadcasted_iota(jnp.int32, (frames, 128), 0)
            row_ref[a] = jnp.where(row < meta[3 * total + a], row_ref[a] + jnp.log(jnp.maximum(acc[a], 1e-30)), 0.0)

    for a in range(2):
        row = lax.broadcasted_iota(jnp.int32, (frames, 128), 0)
        pos = s_ref[a].astype(F32) * t_buf[a * tiles, :, :width].astype(F32)
        terms = jnp.where(row < meta[3 * total + a], row_ref[a] * (1.0 / 128) - (2.0 * scale) * pos, 0.0)
        sum_ref[...] += jnp.sum(terms.reshape(frames // 8, 8, 128), axis=0)


def first_pass(meta, student, every, n_dp, tiles, step=512):
    blocks, frames, width = student.shape
    total = blocks * tiles
    smem, vmem = pl.BlockSpec(memory_space=pltpu.SMEM), pl.BlockSpec(memory_space=pltpu.VMEM)
    return pl.pallas_call(
        functools.partial(first_kernel, tiles, step),
        out_shape=(
            jax.ShapeDtypeStruct((blocks, frames, 128), F32),
            jax.ShapeDtypeStruct((n_dp, 8, 128), F32),
            jax.ShapeDtypeStruct((blocks, 8, 128), F32),
            jax.ShapeDtypeStruct((1,), jnp.int32),
            jax.ShapeDtypeStruct((8, 128), F32),
        ),
        in_specs=[smem, vmem, pl.BlockSpec(memory_space=pl.ANY)],
        out_specs=(vmem, vmem, vmem, smem, vmem),
        scratch_shapes=[
            pltpu.VMEM((total, frames, 2 * width), jnp.bfloat16),
            pltpu.VMEM((blocks, frames, 2 * width), jnp.bfloat16),
            pltpu.VMEM((blocks, frames, 128), F32),
            pltpu.VMEM((8, frames), F32),
            pltpu.SemaphoreType.DMA((total,)),
        ],
        name="first_pass",
    )(meta, student, every)


def second_kernel(tiles, step, meta, ok_ref, s_ref, every, row_ref, far_ref, own_ref, out_ref, t_buf, s_buf, w_buf, acc, sems):
    frames, width = s_ref.shape[1], s_ref.shape[2]
    total = 2 * tiles
    c2 = 1.0 / math.sqrt(width) / math.log(2.0)
    scale = 1.0 / math.sqrt(width)
    for e in range(total):
        fetch(meta, every, t_buf, sems, e).start()
    for a in range(2):
        s_buf[a, :, :width] = s_ref[a]
        augment(s_buf, a, meta[3 * total + a], False)
    acc[...] = jnp.zeros_like(acc)

    def lse_row(e, r):
        a, k = e // tiles, e % tiles
        far = far_ref[meta[2 * total + e], r:r + 1, :]
        return jnp.where(k == 0, own_ref[a, r:r + 1, :], far)

    def tile(e, carry):
        a = e // tiles
        keys = meta[total + e]
        fetch(meta, every, t_buf, sems, e).wait()
        augment(t_buf, e, keys, True)
        chunks = (meta[3 * total + a] + step - 1) // step
        spans = (keys + STEP - 1) // STEP
        for r in range(frames // 128):
            rows = slice(r * 128, (r + 1) * 128)
            weight = jnp.broadcast_to(0.5 * jnp.exp(-lse_row(e, r)), (128, 128)).T
            t = t_buf[e, rows, :width]
            w_buf[rows, :width] = t
            inside = lax.broadcasted_iota(jnp.int32, (128, 128), 0) + r * 128 < keys
            w_buf[rows, width:] = jnp.where(inside, weight * t.astype(F32), 0.0).astype(w_buf.dtype)
        for v in range(1, frames // STEP + 1):
            @pl.when(spans == v)
            def _():
                def chunk(i, c):
                    rows = pl.ds(pl.multiple_of(i * step, step), step)
                    lhs = s_buf[a, rows, :]
                    part = acc[a, rows, :]
                    for j in range(v):
                        cols = slice(j * STEP, (j + 1) * STEP)
                        p = jnp.exp2(nt(lhs, t_buf[e, cols, :]) * c2).astype(jnp.bfloat16)
                        part = part + jnp.dot(p, w_buf[cols, :], preferred_element_type=F32)
                    acc[a, rows, :] = part
                    return c
                lax.fori_loop(0, chunks, chunk, 0)
        return carry

    @pl.when(ok_ref[0] != 0)
    def _():
        lax.fori_loop(0, total, tile, 0)

    @pl.when(ok_ref[0] == 0)
    def _():
        half = 128

        def slow_tile(e, carry):
            a = e // tiles
            fetch(meta, every, t_buf, sems, e).wait()
            augment(t_buf, e, meta[total + e], True)

            def slow_chunk(i, c):
                rows = pl.ds(pl.multiple_of(i * half, half), half)
                lhs = s_buf[a, rows, :]
                part = acc[a, rows, width:]
                for j in range(frames // half):
                    cols = slice(j * half, (j + 1) * half)
                    sc = nt(lhs, t_buf[e, cols, :]) * scale
                    g = 0.5 * (jnp.exp(sc - row_ref[a, rows, :]) + jnp.exp(sc - lse_row(e, j)))
                    g = jnp.where(sc > -0.01 * BIG, g, 0.0)
                    part = part + jnp.dot(g.astype(jnp.bfloat16), t_buf[e, cols, :width], preferred_element_type=F32)
                acc[a, rows, width:] = part
                return c
            lax.fori_loop(0, frames // half, slow_chunk, 0)
            return carry
        lax.fori_loop(0, total, slow_tile, 0)

    for a in range(2):
        row = lax.broadcasted_iota(jnp.int32, (frames, width), 0)
        scaled = 0.5 * jnp.exp(-row_ref[a]) * acc[a, :, :width]
        grad = jnp.where(ok_ref[0] != 0, scaled, 0.0) + acc[a, :, width:] - t_buf[a * tiles, :, :width].astype(F32)
        out_ref[a] = jnp.where(row < meta[3 * total + a], grad * scale, 0.0).astype(out_ref.dtype)


def second_pass(meta, ok, student, every, rows, far, own, tiles, step=512):
    blocks, frames, width = student.shape
    total = blocks * tiles
    smem, vmem = pl.BlockSpec(memory_space=pltpu.SMEM), pl.BlockSpec(memory_space=pltpu.VMEM)
    return pl.pallas_call(
        functools.partial(second_kernel, tiles, step),
        out_shape=jax.ShapeDtypeStruct(student.shape, student.dtype),
        in_specs=[smem, smem, vmem, pl.BlockSpec(memory_space=pl.ANY), vmem, vmem, vmem],
        out_specs=vmem,
        scratch_shapes=[
            pltpu.VMEM((total, frames, 2 * width), jnp.bfloat16),
            pltpu.VMEM((blocks, frames, 2 * width), jnp.bfloat16),
            pltpu.VMEM((frames, 2 * width), jnp.bfloat16),
            pltpu.VMEM((blocks, frames, 2 * width), F32),
            pltpu.SemaphoreType.DMA((total,)),
        ],
        name="second_pass",
    )(meta, ok, student, every, rows, far, own)


def exchange_kernel(n_dp, n_tm, bias_ref, pick_ref, count_ref, send_ref, own_ref, sum_ref, far_ref, lse_ref, loss_ref,
                    inc, reply, side, column, s1, r1, s2, r2, s3, r3, s4, r4):
    me, tm = lax.axis_index("dp"), lax.axis_index("tm")
    barrier = pltpu.get_barrier_semaphore()

    def greet(o, c):
        pl.semaphore_signal(barrier, inc=1, device_id=((me + o) % n_dp, tm), device_id_type=MESH)
        return c
    lax.fori_loop(1, n_dp, greet, 0)
    for o in range(1, n_tm):
        pl.semaphore_signal(barrier, inc=1, device_id=(me, (tm + o) % n_tm), device_id_type=MESH)
    inc[me] = send_ref[me]
    pl.semaphore_wait(barrier, n_dp - 1 + n_tm - 1)

    def ask(o):
        to = (me + o) % n_dp
        return pltpu.make_async_remote_copy(
            src_ref=send_ref.at[to], dst_ref=inc.at[me], send_sem=s1.at[o], recv_sem=r1.at[o],
            device_id=(to, tm), device_id_type=MESH)

    def answer(o):
        to = (me + o) % n_dp
        return pltpu.make_async_remote_copy(
            src_ref=reply.at[to], dst_ref=far_ref.at[me], send_sem=s2.at[o], recv_sem=r2.at[o],
            device_id=(to, tm), device_id_type=MESH)

    def tell(o):
        return pltpu.make_async_remote_copy(
            src_ref=column.at[me], dst_ref=column.at[me], send_sem=s4.at[o], recv_sem=r4.at[o],
            device_id=((me + o) % n_dp, tm), device_id_type=MESH)

    def beside(o):
        return pltpu.make_async_remote_copy(
            src_ref=side.at[tm], dst_ref=side.at[tm], send_sem=s3.at[o], recv_sem=r3.at[o],
            device_id=(me, (tm + o) % n_tm), device_id_type=MESH)

    def each(f):
        def step(o, c):
            f(o)
            return c
        lax.fori_loop(1, n_dp, step, 0)

    each(lambda o: ask(o).start())
    each(lambda o: ask(o).wait_recv())
    terms = sum_ref[...]
    frame = lax.broadcasted_iota(jnp.int32, (8, 128), 0) * 128 + lax.broadcasted_iota(jnp.int32, (8, 128), 1)
    for a in range(2):
        best = own_ref[a]
        for p in range(n_dp):
            best = jnp.maximum(best, inc[p] + bias_ref[a, p])
        total = jnp.exp(own_ref[a] - best)
        for p in range(n_dp):
            total = total + jnp.exp(inc[p] + bias_ref[a, p] - best)
        lse = best + jnp.log(total)
        lse = jnp.where(frame < count_ref[a], lse, 0.0)
        lse_ref[a] = lse
        terms = terms + lse
    side[tm] = terms
    for p in range(n_dp):
        share = pick_ref[p]
        reply[p] = lse_ref[0] * (1.0 - share) + lse_ref[1] * share
    far_ref[me] = reply[me]
    each(lambda o: answer(o).start())
    for o in range(1, n_tm):
        beside(o).start()
    for o in range(1, n_tm):
        beside(o).wait_recv()
    rows = side[0]
    for t in range(1, n_tm):
        rows = rows + side[t]
    column[me] = rows
    each(lambda o: tell(o).start())
    each(lambda o: answer(o).wait_recv())
    each(lambda o: tell(o).wait_recv())
    rows = column[0]
    for p in range(1, n_dp):
        rows = rows + column[p]
    loss_ref[0] = 0.5 * jnp.sum(rows)
    each(lambda o: ask(o).wait_send())
    each(lambda o: answer(o).wait_send())
    each(lambda o: tell(o).wait_send())
    for o in range(1, n_tm):
        beside(o).wait_send()


def exchange(bias, pick, count, send, own, sums, n_tm):
    n_dp = send.shape[0]
    smem, vmem = pl.BlockSpec(memory_space=pltpu.SMEM), pl.BlockSpec(memory_space=pltpu.VMEM)
    dma = pltpu.SemaphoreType.DMA
    return pl.pallas_call(
        functools.partial(exchange_kernel, n_dp, n_tm),
        out_shape=(
            jax.ShapeDtypeStruct((n_dp, 8, 128), F32),
            jax.ShapeDtypeStruct((2, 8, 128), F32),
            jax.ShapeDtypeStruct((1,), F32),
        ),
        in_specs=[smem, smem, smem, vmem, vmem, vmem],
        out_specs=(vmem, vmem, smem),
        scratch_shapes=[
            pltpu.VMEM((n_dp, 8, 128), F32), pltpu.VMEM((n_dp, 8, 128), F32),
            pltpu.VMEM((n_tm, 8, 128), F32), pltpu.VMEM((n_dp, 8, 128), F32),
            dma((n_dp,)), dma((n_dp,)), dma((n_dp,)), dma((n_dp,)),
            dma((n_tm,)), dma((n_tm,)), dma((n_dp,)), dma((n_dp,)),
        ],
        compiler_params=pltpu.CompilerParams(collective_id=1, has_side_effects=True),
        name="exchange",
    )(bias, pick, count, send, own, sums)


def body(student, teacher, partner_dp, partner_slot, valid_frames):
    n_dp, n_tm = lax.axis_size("dp"), lax.axis_size("tm")
    me, tm = lax.axis_index("dp"), lax.axis_index("tm")
    blocks, frames, width = student.shape
    k = partner_dp.shape[1]
    entries = blocks * k
    dest_all = lax.dynamic_index_in_dim(partner_dp.reshape(n_dp, n_tm, entries), tm, 1, keepdims=False)
    slot_all = lax.dynamic_index_in_dim(partner_slot.reshape(n_dp, n_tm, entries), tm, 1, keepdims=False)
    lens = lax.dynamic_index_in_dim(valid_frames.reshape(n_dp, n_tm, blocks), tm, 1, keepdims=False)
    dest = lax.dynamic_index_in_dim(dest_all, me, 0, keepdims=False).reshape(blocks, k)
    slot = lax.dynamic_index_in_dim(slot_all, me, 0, keepdims=False).reshape(blocks, k)
    own = me * blocks + jnp.arange(blocks, dtype=jnp.int32)
    ids = jnp.concatenate([own[:, None], dest * blocks + slot], axis=1).reshape(-1)
    flat_lens = lens.reshape(-1)
    goes = jnp.concatenate([jnp.zeros((blocks, 1), jnp.int32), dest], axis=1).reshape(-1)
    count = lax.dynamic_index_in_dim(lens, me, 0, keepdims=False)
    meta = jnp.concatenate([ids, flat_lens[ids], goes, count])
    wanted = dest_all == me
    asked = jnp.max(jnp.where(wanted, slot_all, -1), axis=1)
    bias = jnp.where(asked[None] == jnp.arange(blocks, dtype=jnp.int32)[:, None], 0.0, -BIG).astype(F32)
    pick = jnp.maximum(asked, 0).astype(F32)

    every = gather(teacher, n_dp).reshape(n_dp * blocks, frames, width)
    rows, send, own_lse, ok, sums = first_pass(meta, student, every, n_dp, k + 1)
    far, lse, loss_sum = exchange(bias, pick, count, send, own_lse, sums, n_tm)
    grad = second_pass(meta, ok, student, every, rows, far, lse, k + 1)
    loss = loss_sum[0] / jnp.sum(valid_frames).astype(F32)
    return (loss, grad)


def solution(mesh):
    placed = (P(("dp", "tm"), None, None), P(("dp", "tm"), None, None), P(), P(), P())
    return jax.shard_map(
        body,
        mesh=mesh,
        in_specs=placed,
        out_specs=(P(), P(("dp", "tm"), None, None)),
        check_vma=False,
    )
```

time: 387 us -> 399 us (1.031)
  Pallas kernels: 0 us -> 386 us
  matrix products: 106 us -> 0 us
  waiting for transfers between devices: 90.8 us -> 0 us
  blocking collectives: 62.7 us -> 0 us
  other arithmetic: 58.2 us -> 3.86 us
  local copies, waits for them, and re-layouts: 27.6 us -> 4.06 us
  between operations: 18.1 us -> 3.11 us
  starting transfers between devices: 13.7 us -> 0 us
  loops' own time: 6.51 us -> 0 us
    pallas_call x0 -> x4, Pallas kernels: none -> 386 us  [the longest x1 195 us: first_pass(): pl.pallas_call(functools.partial(first_kernel, tiles, step), out_shape=(j...]
    dot_general x18 -> x0, matrix products: 106 us -> none  [the longest x9 74.6 us: second_pass(): jnp.einsum('aij,aje->aie', grad_scores.astype(jnp.bfloat16), key_block, p...]
    all_gather x1 -> x0, waiting for transfers between devices: 70.4 us -> none  [body(): everyone = lax.all_gather(teacher, 'dp', axis=0, tiled=True)]
    psum x1 -> x0, blocking collectives: 62.7 us -> none  [body(): loss_sum = lax.psum(0.5 * (row_terms + col_terms), ('dp', 'tm'))]
    reduce_sum x17 -> x1, other arithmetic: 49.1 us -> 1.32 us  [body(): loss = loss_sum[0] / jnp.sum(valid_frames).astype(F32)]
    all_to_all x3 -> x0, waiting for transfers between devices: 19.7 us -> none  [the longest x1 7.55 us: body(): lax.all_to_all(back_sum, 'dp', split_axis=0, concat_axis=0, tiled=True)]
    all_to_all x3 -> x0, starting transfers between devices: 13.7 us -> none  [the longest x1 5.41 us: body(): lax.all_to_all(back_best, 'dp', split_axis=0, concat_axis=0, tiled=True)]
    gather x4 -> x1, local copies, waits for them, and re-layouts: 11.3 us -> 0.7 us  [body(): meta = jnp.concatenate([ids, flat_lens[ids], goes, count])]
  transfers between devices with their start and end apart: 4 -> 0, of which waited for: 4 -> 0; matrix products, arithmetic and copies ran while one was open for 2% -> 0% of each run, Pallas kernels for 0% -> 0%
where the time goes in v1:
time: 399 us; the launch traced here: 397 us
  Pallas kernels  386 us (97%)
  local copies, waits for them, and re-layouts  4.06 us (1%)
    pallas_call x1, Pallas kernels, first_pass(): pl.pallas_call(functools.partial(first_kernel, tiles, step), out_shape=(j...  195 us
    pallas_call x1, Pallas kernels, second_pass(): pl.pallas_call(functools.partial(second_kernel, tiles, step), out_shape=j...  115 us
    pallas_call x1, Pallas kernels, gather(): pl.pallas_call(functools.partial(gather_kernel, rows), out_shape=jax.Shap...  55.5 us
    pallas_call x1, Pallas kernels, exchange(): pl.pallas_call(functools.partial(exchange_kernel, n_dp, n_tm), out_shape=...  20.7 us

profile of v1, /device:TPU:7, one launch (start us, length us, event | category | flops | bytes accessed | tf_op | source)
XLA Modules:
  0.0 396.7 jit_solution(5887803606247172493)
XLA Ops:
  0.6 1.3 reduce_sum.9
  2.6 0.8 reshape.84
  3.5 0.0 copy-start
  3.5 0.1 dynamic-slice_reduce_fusion
  3.6 0.1 reshape.88
  3.7 0.8 copy.7
  4.5 0.1 reshape.82
  4.6 0.8 copy.8
  5.4 0.1 reshape.83
  5.5 0.7 fusion
  6.3 0.1 reshape.85
  6.3 0.5 maximum_convert_fusion.pick_ref
  6.9 0.6 compare_select_fusion.2.bias_ref
  7.4 0.1 concatenate.10
  7.5 0.1 reshape.90
  7.6 0.1 reshape.86
  7.7 0.1 pad_add_fusion
  7.7 0.1 reshape.89
  7.8 0.1 reshape.87
  7.9 0.7 gather_fusion
  8.6 0.7 pad_add_fusion.1.meta
  9.3 55.5 %gather.7 = bf16[32,2,1024,128]{3,2,1,0:T(8,128)(2,1)} custom-call(bf16[2,1024,128]{2,1,0:T(8,128)(2,1)} %t_ref.1), custom_call_target="tpu_custom_call" | custom-call | tf_op jit(solution)/shard_map/gather/pallas_call | solution.py:169
  64.8 194.6 %first_pass.1 = (f32[2,1024,128]{2,1,0:T(8,128)}, f32[32,8,128]{2,1,0:T(8,128)}, f32[2,8,128]{2,1,0:T(8,128)}, s32[1]{0:T(128)}, f32[8,128]{1,0:T(8,128)}) custom-call(s32[56]{0:T(128)} %pad_add_fusion.1.meta, bf16[2,1024,128]{2,1,0:T(8,128)(2,1)} %s_ref.3, bf16[64,1024,128]{2,1,0:T(8,128)(2,1)} %bitcast.6), custom_call_target="tpu_custom_call" | custom-call | tf_op jit(solution)/shard_map/first_pass/pallas_call | solution.py:330
  259.4 0.0 copy-done
  259.4 20.7 %exchange.1 = (f32[32,8,128]{2,1,0:T(8,128)}, f32[2,8,128]{2,1,0:T(8,128)}, f32[1]{0:T(128)}) custom-call(f32[2,32]{1,0:T(2,128)} %compare_select_fusion.2.bias_ref, f32[32]{0:T(128)} %maximum_convert_fusion.pick_ref, s32[2]{0:T(128)} %copy-done, f32[32,8,128]{2,1,0:T(8,128)} %get-tuple-element.10.send_ref, f32[2,8,128]{2,1,0:T(8,128)} %get-tuple-element.11.own_ref, ...), custom_call_target="tpu_custom_call" | custom-call | tf_op jit(solution)/shard_map/exchange/pallas_call | solution.py:544
  280.7 114.9 %second_pass.1 = bf16[2,1024,128]{2,1,0:T(8,128)(2,1)} custom-call(s32[56]{0:T(128)} %pad_add_fusion.1.meta, s32[1]{0:T(128)} %get-tuple-element.14.ok_ref, bf16[2,1024,128]{2,1,0:T(8,128)(2,1)} %s_ref.3, bf16[64,1024,128]{2,1,0:T(8,128)(2,1)} %bitcast.7, f32[2,1024,128]{2,1,0:T(8,128)} %get-tuple-element.15.row_ref, ...), custom_call_target="tpu_custom_call" | custom-call | tf_op jit(solution)/shard_map/second_pass/pallas_call | solution.py:439
  (6 shorter events, 0.1 us)
Async XLA Ops:
  3.5 255.9 %copy-start = (s32[2]{0:T(128)}, s32[2]{0:T(128)S(1)}, u32[]{:S(2)}) copy-start(s32[2]{0:T(128)S(1)} %fusion.1.count_ref) | copy-start | bytes 28

commit v2 on v1

v2 whole, which is shorter than its diff:
```python
import functools
import heapq
import math

import jax
import jax.numpy as jnp
from jax import lax
from jax.experimental import pallas as pl
from jax.experimental.pallas import tpu as pltpu
from jax.sharding import PartitionSpec as P

MESH = pl.DeviceIdType.MESH
F32 = jnp.float32
BIG = 1e30

ZP, ZM, YP, YM = range(4)
MOVE = {ZP: (1, 0), ZM: (-1, 0), YP: (0, 1), YM: (0, -1)}


PARTS = 2


def onward(tile, oz, oy, part):
    half = part * 2 // PARTS
    first, second = (oz, oy) if tile == 0 else (oy, oz)
    plus1, minus1 = (ZP, ZM) if tile == 0 else (YP, YM)
    plus2, minus2 = (YP, YM) if tile == 0 else (ZP, ZM)
    links = []
    if second == 0:
        if first == 0:
            links += [plus1, minus1]
        elif first == 1 and half == 0:
            links += [plus1]
        elif first == 3 and half == 1:
            links += [minus1]
        links += [plus2, minus2]
    elif second == 1 and half == 0:
        links += [plus2]
    elif second == 3 and half == 1:
        links += [minus2]
    return links


def moved(oz, oy, link):
    dz, dy = MOVE[link]
    return (oz + dz) % 4, (oy + dy) % 4


def plan():
    free = [0.0] * 4
    events, order, count = [], [], 0

    def send(unit, link, now):
        nonlocal count
        tile, oz, oy, half = unit
        start = max(now, free[link])
        free[link] = start + 1.0
        noz, noy = moved(oz, oy, link)
        heapq.heappush(events, (free[link] + 0.5, count, (tile, noz, noy, half), link))
        count += 1

    first = []
    for link in range(4):
        near = 0 if link in (ZP, ZM) else 1
        lead = 0 if link in (ZP, YP) else 1
        for tile in (near, 1 - near):
            for part in range(PARTS):
                first.append(((tile, 0, 0, part if lead == 0 else PARTS - 1 - part), link))
    first = [first[k * 2 * PARTS + i] for i in range(2 * PARTS) for k in range(4)]
    for unit, link in first:
        send(unit, link, 0.0)
    while events:
        now, _, unit, _ = heapq.heappop(events)
        out = onward(*unit)
        order.append((unit, out))
        for link in out:
            send(unit, link, now)
    return first, order, max(free)


def lay_requests(me, tm, n_tm, dp_ref, slot_ref, ask_ref):
    asked = jnp.max(jnp.where(dp_ref[...] == me, slot_ref[...], -1).astype(F32), axis=0, keepdims=True)
    lane = lax.broadcasted_iota(jnp.int32, asked.shape, 1) // 2
    for p in range(ask_ref.shape[0]):
        one = jnp.max(jnp.where(lane == p * n_tm + tm, asked, -1.0), axis=1, keepdims=True)
        one = jnp.broadcast_to(one, (8, 128))
        ask_ref[p, 0] = jnp.where(one == 0.0, 0.0, -BIG)
        ask_ref[p, 1] = jnp.where(one == 1.0, 0.0, -BIG)
        ask_ref[p, 2] = jnp.maximum(one, 0.0)


def lay_side(me, tm, n_tm, t_ref, s_ref, valid_ref, side_ref):
    blocks, frames, width = t_ref.shape
    row = lax.broadcasted_iota(jnp.int32, (frames, width), 0)
    total = jnp.zeros((8, width), F32)
    for a in range(blocks):
        both = s_ref[a].astype(F32) * t_ref[a].astype(F32)
        both = jnp.where(row < valid_ref[(me * n_tm + tm) * blocks + a], both, 0.0)
        total = total + jnp.sum(both.reshape(frames // 8, 8, width), axis=0)
    side_ref[0] = total * (-2.0 / math.sqrt(width))
    count = lax.fori_loop(0, valid_ref.shape[0], lambda i, c: c + valid_ref[i], jnp.int32(0))
    side_ref[1] = jnp.full((8, width), count).astype(F32)


def gather_kernel(rows, n_tm, t_ref, s_ref, dp_ref, slot_ref, valid_ref, out_ref, ask_ref, side_ref,
                  send_sem, recv_sem, peer_send, peer_recv, own_sem):
    half_rows = rows // PARTS
    me, tm = lax.axis_index("dp"), lax.axis_index("tm")
    z, y, c = me // 8, (me // 2) % 4, me % 2

    def dp_of(zz, yy, cc):
        return (zz * 4 + yy) * 2 + cc

    near = [
        dp_of((z + 1) % 4, y, c), dp_of((z + 3) % 4, y, c),
        dp_of(z, (y + 1) % 4, c), dp_of(z, (y + 3) % 4, c),
    ]
    peer = dp_of(z, y, 1 - c)
    barrier = pltpu.get_barrier_semaphore()
    for other in near + [peer]:
        pl.semaphore_signal(barrier, inc=1, device_id=(other, tm), device_id_type=MESH)
    pl.semaphore_wait(barrier, 5)

    first, order, _ = plan()
    sends = []

    def recv_id(unit):
        tile, oz, oy, half = unit
        return ((tile * 4 + oz) * 4 + oy) * PARTS + half

    def slot(unit):
        _, oz, oy, _ = unit
        return dp_of((z + 4 - oz) % 4, (y + 4 - oy) % 4, c)

    def place(ref, unit):
        tile, oz, oy, half = unit
        return ref.at[slot(unit), tile, pl.ds(half * half_rows, half_rows)]

    def source(unit):
        tile, oz, oy, half = unit
        if oz == 0 and oy == 0:
            return t_ref.at[tile, pl.ds(half * half_rows, half_rows)]
        return place(out_ref, unit)

    def send(unit, link):
        tile, oz, oy, half = unit
        copy = pltpu.make_async_remote_copy(
            src_ref=source(unit), dst_ref=place(out_ref, unit),
            send_sem=send_sem.at[len(sends)], recv_sem=recv_sem.at[recv_id((tile, *moved(oz, oy, link), half))],
            device_id=(near[link], tm), device_id_type=MESH,
        )
        copy.start()
        sends.append(copy)

    shares = []

    def share(unit):
        copy = pltpu.make_async_remote_copy(
            src_ref=source(unit), dst_ref=place(out_ref, unit),
            send_sem=peer_send.at[recv_id(unit)], recv_sem=peer_recv.at[recv_id(unit)],
            device_id=(peer, tm), device_id_type=MESH,
        )
        copy.start()
        shares.append(copy)

    for unit, link in first:
        send(unit, link)
    for tile in (0, 1):
        for half in range(PARTS):
            share((tile, 0, 0, half))
    own = pltpu.make_async_copy(t_ref, out_ref.at[me], own_sem)
    own.start()
    lay_requests(me, tm, n_tm, dp_ref, slot_ref, ask_ref)
    lay_side(me, tm, n_tm, t_ref, s_ref, valid_ref, side_ref)
    for unit, out in order:
        here = place(out_ref, unit)
        pltpu.make_async_remote_copy(
            src_ref=here, dst_ref=here, send_sem=send_sem.at[0], recv_sem=recv_sem.at[recv_id(unit)],
            device_id=(near[0], tm), device_id_type=MESH,
        ).wait_recv()
        for link in out:
            send(unit, link)
        share(unit)
    for copy in shares:
        copy.wait_send()
        copy.wait_recv()
    for copy in sends:
        copy.wait_send()
    own.wait()


def gather(teacher, student, tables, n_dp, n_tm):
    blocks, rows, width = teacher.shape
    smem, vmem, far = (pl.BlockSpec(memory_space=m) for m in (pltpu.SMEM, pltpu.VMEM, pl.ANY))
    first, order, _ = plan()
    n_sends = len(first) + sum(len(o) for _, o in order)
    return pl.pallas_call(
        functools.partial(gather_kernel, rows, n_tm),
        out_shape=(
            jax.ShapeDtypeStruct((n_dp, blocks, rows, width), teacher.dtype),
            jax.ShapeDtypeStruct((n_dp, 3, 8, 128), F32),
            jax.ShapeDtypeStruct((2, 8, 128), F32),
        ),
        in_specs=[vmem, vmem, vmem, vmem, smem],
        out_specs=(far, vmem, vmem),
        scratch_shapes=[
            pltpu.SemaphoreType.DMA((n_sends,)), pltpu.SemaphoreType.DMA((32 * PARTS,)),
            pltpu.SemaphoreType.DMA((32 * PARTS,)), pltpu.SemaphoreType.DMA((32 * PARTS,)), pltpu.SemaphoreType.DMA,
        ],
        compiler_params=pltpu.CompilerParams(collective_id=0, has_side_effects=True),
        name="gather",
    )(teacher, student, *tables)


LOW, HIGH = 2.0 ** -60, 2.0 ** 100
SPAN = 256
UNIT = 256


def lay_table(meta, tiles, me, tm, n_tm, dp_ref, slot_ref, valid_ref):
    for a in range(2):
        mine = (me * n_tm + tm) * 2 + a
        meta[3, a] = valid_ref[mine]
        meta[0, a * tiles] = me * 2 + a
        meta[1, a * tiles] = valid_ref[mine]
        meta[2, a * tiles] = 0
        for k in range(1, tiles):
            far, slot = dp_ref[k - 1, mine], slot_ref[k - 1, mine]
            meta[0, a * tiles + k] = far * 2 + slot
            meta[1, a * tiles + k] = valid_ref[(far * n_tm + tm) * 2 + slot]
            meta[2, a * tiles + k] = far


def edge(shape, start, count, key):
    row = lax.broadcasted_iota(jnp.int32, shape, 0) + start
    lane = lax.broadcasted_iota(jnp.int32, shape, 1)
    mine, other = (0, 1) if key else (1, 0)
    return jnp.where(lane == mine, jnp.where(row < count, 0.0, -BIG), jnp.where(lane == other, 1.0, 0.0)).astype(jnp.bfloat16)


def nt(a, b):
    return lax.dot_general(a, b, (((1,), (1,)), ((), ())), preferred_element_type=F32)


def ceil_of(x, n):
    return (x + n - 1) // n


def stash(e, u, v, inside, outside, sems, out):
    rows = pl.ds(pl.multiple_of(u * UNIT, UNIT), UNIT)
    near, far = inside.at[e, pl.ds(0, v), rows], outside.at[e, pl.ds(0, v), rows]
    return pltpu.make_async_copy(near, far, sems.at[e, u]) if out else pltpu.make_async_copy(far, near, sems.at[e, u])


def first_kernel(tiles, n_tm, dp_ref, slot_ref, valid_ref, s_ref, every, row_ref, send_ref, own_ref, ok_ref, sum_ref, e_hbm,
                 t_buf, right, key_edge, key_full, acc, col, ends, e_buf, meta, sems, e_sems):
    me, tm = lax.axis_index("dp"), lax.axis_index("tm")
    frames, width = s_ref.shape[1], s_ref.shape[2]
    total = 2 * tiles
    spans_most = frames // SPAN
    scale = 1.0 / math.sqrt(width)
    c2 = scale / math.log(2.0)
    lay_table(meta, tiles, me, tm, n_tm, dp_ref, slot_ref, valid_ref)

    def fetch(e):
        return pltpu.make_async_copy(every.at[meta[0, e]], t_buf.at[e], sems.at[e])
    for e in range(total):
        fetch(e).start()
    for a in range(2):
        right[a] = edge((frames, width), 0, meta[3, a], False)
    key_full[...] = edge((SPAN, width), 0, SPAN, True)
    acc[...] = jnp.zeros_like(acc)
    ok_ref[0] = 1
    sum_ref[...] = jnp.zeros_like(sum_ref)
    ends[...] = jnp.ones_like(ends)
    lane = lax.broadcasted_iota(jnp.int32, (1, frames), 1)
    send_ref[...] = jnp.zeros_like(send_ref)

    def put(e, values):
        a, k = e // tiles, e % tiles

        @pl.when(k == 0)
        def _():
            for r in range(8):
                own_ref[a, r:r + 1, :] = values[:, r * 128:(r + 1) * 128]

        @pl.when(k != 0)
        def _():
            for r in range(8):
                send_ref[meta[2, e], r:r + 1, :] = values[:, r * 128:(r + 1) * 128]

    def by_spans(e, run):
        spans = ceil_of(meta[1, e], SPAN)
        for v in range(1, spans_most + 1):
            pl.when(spans == v)(functools.partial(run, v))

    def tile(e, carry):
        a = e // tiles
        keys = meta[1, e]
        fetch(e).wait()
        col[...] = jnp.zeros_like(col)
        units = ceil_of(meta[3, a], UNIT)
        key_edge[...] = edge((SPAN, width), (ceil_of(keys, SPAN) - 1) * SPAN, keys, True)

        def run(v):
            def piece(u, many):
                n = UNIT * many
                rows = pl.ds(pl.multiple_of(u * UNIT, UNIT), n)
                lhs = jnp.concatenate([s_ref[a, rows, :], right[a, rows, :]], axis=1)
                part = acc[a, rows, :]
                for j in range(v):
                    cols = slice(j * SPAN, (j + 1) * SPAN)
                    side = key_edge if j == v - 1 else key_full
                    rhs = jnp.concatenate([t_buf[e, cols, :], side[...]], axis=1)
                    p = jnp.exp2(nt(lhs, rhs) * c2)
                    e_buf[e, j, rows, :] = p.astype(jnp.bfloat16)
                    for w in range(SPAN // 128):
                        part = part + p[:, w * 128:(w + 1) * 128]
                    col[:, cols] += jnp.sum(p.reshape(n // 8, 8, SPAN), axis=0)
                acc[a, rows, :] = part
                for i in range(many):
                    stash(e, u + i, v, e_buf, e_hbm, e_sems, True).start()

            def pair(i, c):
                piece(2 * i, 2)
                return c
            lax.fori_loop(0, units // 2, pair, 0)
            pl.when(units % 2 == 1)(lambda: piece(units - 1, 1))
        by_spans(e, run)
        sums = jnp.sum(col[...], axis=0, keepdims=True)
        sums = jnp.where(lane < keys, sums, 1.0)
        ends[0:1, :] = jnp.minimum(ends[0:1, :], sums)
        ends[1:2, :] = jnp.maximum(ends[1:2, :], sums)
        put(e, jnp.where(lane < keys, jnp.log(sums), -BIG))
        return carry

    lax.fori_loop(0, total, tile, 0)

    low, high = jnp.min(ends[0:1, :]), jnp.max(ends[1:2, :])
    row = lax.broadcasted_iota(jnp.int32, (frames, 128), 0)
    for a in range(2):
        sums = jnp.broadcast_to(jnp.sum(acc[a], axis=1, keepdims=True), (frames, 128))
        sums = jnp.where(row < meta[3, a], sums, 1.0)
        low, high = jnp.minimum(low, jnp.min(sums)), jnp.maximum(high, jnp.max(sums))
        lse = jnp.log(sums)
        row_ref[a] = lse
        sum_ref[...] += jnp.sum(lse.reshape(frames // 8, 8, 128), axis=0)

    @pl.when(jnp.logical_not((low >= LOW) & (high <= HIGH)))
    def _():
        ok_ref[0] = 0
        row_ref[...] = jnp.full(row_ref.shape, -BIG, F32)
        acc[...] = jnp.zeros_like(acc)
        sum_ref[...] = jnp.zeros_like(sum_ref)
        half = 128

        def slow_tile(e, carry):
            a = e // tiles
            keys = meta[1, e]
            col[0:1, :] = jnp.full((1, frames), -BIG, F32)
            col[1:2, :] = jnp.zeros((1, frames), F32)

            def slow_chunk(i, c):
                rows = pl.ds(pl.multiple_of(i * half, half), half)
                lhs = jnp.concatenate([s_ref[a, rows, :], right[a, rows, :]], axis=1)
                for j in range(frames // half):
                    cols = slice(j * half, (j + 1) * half)
                    rhs = jnp.concatenate([t_buf[e, cols, :], edge((half, width), j * half, keys, True)], axis=1)
                    sc = nt(lhs, rhs) * scale
                    old = row_ref[a, rows, :]
                    new = jnp.maximum(old, jnp.broadcast_to(jnp.max(sc, axis=1, keepdims=True), (half, 128)))
                    acc[a, rows, :] = acc[a, rows, :] * jnp.exp(old - new) + jnp.broadcast_to(
                        jnp.sum(jnp.where(sc > -0.01 * BIG, jnp.exp(sc - new[:, :1]), 0.0), axis=1, keepdims=True), (half, 128))
                    row_ref[a, rows, :] = new
                    cold = col[0:1, cols]
                    cnew = jnp.maximum(cold, jnp.max(sc, axis=0, keepdims=True))
                    col[1:2, cols] = col[1:2, cols] * jnp.exp(cold - cnew) + jnp.sum(
                        jnp.where(sc > -0.01 * BIG, jnp.exp(sc - cnew), 0.0), axis=0, keepdims=True)
                    col[0:1, cols] = cnew
                return c
            lax.fori_loop(0, frames // half, slow_chunk, 0)
            real = lane < keys
            put(e, jnp.where(real, col[0:1, :] + jnp.log(jnp.where(real, col[1:2, :], 1.0)), -BIG))
            return carry
        lax.fori_loop(0, total, slow_tile, 0)
        for a in range(2):
            lse = jnp.where(row < meta[3, a], row_ref[a] + jnp.log(jnp.maximum(acc[a], 1e-30)), 0.0)
            row_ref[a] = lse
            sum_ref[...] += jnp.sum(lse.reshape(frames // 8, 8, 128), axis=0)

    sum_ref[...] = sum_ref[...] * (1.0 / 128)

    def drain(e, carry):
        def run(v):
            def one(u, c):
                stash(e, u, v, e_buf, e_hbm, e_sems, True).wait()
                return c
            lax.fori_loop(0, ceil_of(meta[3, e // tiles], UNIT), one, 0)
        by_spans(e, run)
        return carry
    lax.fori_loop(0, total, drain, 0)


def first_pass(tables, student, every, n_dp, n_tm, tiles):
    blocks, frames, width = student.shape
    total = blocks * tiles
    smem, vmem, far = (pl.BlockSpec(memory_space=m) for m in (pltpu.SMEM, pltpu.VMEM, pl.ANY))
    return pl.pallas_call(
        functools.partial(first_kernel, tiles, n_tm),
        out_shape=(
            jax.ShapeDtypeStruct((blocks, frames, 128), F32),
            jax.ShapeDtypeStruct((n_dp, 8, 128), F32),
            jax.ShapeDtypeStruct((blocks, 8, 128), F32),
            jax.ShapeDtypeStruct((1,), jnp.int32),
            jax.ShapeDtypeStruct((8, 128), F32),
            jax.ShapeDtypeStruct((total, frames // SPAN, frames, SPAN), jnp.bfloat16),
        ),
        in_specs=[smem, smem, smem, vmem, far],
        out_specs=(vmem, vmem, vmem, smem, vmem, far),
        scratch_shapes=[
            pltpu.VMEM((total, frames, width), jnp.bfloat16),
            pltpu.VMEM((blocks, frames, width), jnp.bfloat16),
            pltpu.VMEM((SPAN, width), jnp.bfloat16),
            pltpu.VMEM((SPAN, width), jnp.bfloat16),
            pltpu.VMEM((blocks, frames, 128), F32),
            pltpu.VMEM((8, frames), F32),
            pltpu.VMEM((8, frames), F32),
            pltpu.VMEM((total, frames // SPAN, frames, SPAN), jnp.bfloat16),
            pltpu.SMEM((4, total), jnp.int32),
            pltpu.SemaphoreType.DMA((total,)),
            pltpu.SemaphoreType.DMA((total, frames // UNIT)),
        ],
        compiler_params=pltpu.CompilerParams(vmem_limit_bytes=60 * 1024 * 1024),
        name="first_pass",
    )(*tables, student, every)


def second_kernel(tiles, n_tm, dp_ref, slot_ref, valid_ref, ok_ref, s_ref, every, e_hbm, row_ref, far_ref, own_ref, out_ref,
                  w_buf, acc, e_buf, meta, sems, e_sems):
    me, tm = lax.axis_index("dp"), lax.axis_index("tm")
    frames, width = s_ref.shape[1], s_ref.shape[2]
    total = 2 * tiles
    spans_most = frames // SPAN
    scale = 1.0 / math.sqrt(width)
    lay_table(meta, tiles, me, tm, n_tm, dp_ref, slot_ref, valid_ref)

    def fetch(e):
        return pltpu.make_async_copy(every.at[meta[0, e]], w_buf.at[e, :, pl.ds(0, width)], sems.at[e])

    def by_spans(e, run):
        spans = ceil_of(meta[1, e], SPAN)
        for v in range(1, spans_most + 1):
            pl.when(spans == v)(functools.partial(run, v))

    def load(e, carry):
        fetch(e).start()

        @pl.when(ok_ref[0] != 0)
        def _():
            def run(v):
                def one(u, c):
                    stash(e, u, v, e_buf, e_hbm, e_sems, False).start()
                    return c
                lax.fori_loop(0, ceil_of(meta[3, e // tiles], UNIT), one, 0)
            by_spans(e, run)
        return carry
    lax.fori_loop(0, total, load, 0)
    acc[...] = jnp.zeros_like(acc)

    def lse_row(e, r):
        a, k = e // tiles, e % tiles
        return jnp.where(k == 0, own_ref[a, r:r + 1, :], far_ref[meta[2, e], r:r + 1, :])

    def tile(e, carry):
        a = e // tiles
        units = ceil_of(meta[3, a], UNIT)
        fetch(e).wait()

        def run(v):
            for r in range(v * SPAN // 128):
                rows = slice(r * 128, (r + 1) * 128)
                weight = jnp.broadcast_to(0.5 * jnp.exp(-lse_row(e, r)), (128, 128)).T
                w_buf[e, rows, width:] = (weight * w_buf[e, rows, :width].astype(F32)).astype(w_buf.dtype)

            def piece(u, many):
                for i in range(many):
                    stash(e, u + i, v, e_buf, e_hbm, e_sems, False).wait()
                rows = pl.ds(pl.multiple_of(u * UNIT, UNIT), UNIT * many)
                lhs = jnp.concatenate([e_buf[e, j, rows, :] for j in range(v)], axis=1)
                acc[a, rows, :] += jnp.dot(lhs, w_buf[e, :v * SPAN, :], preferred_element_type=F32)

            def pair(i, c):
                piece(2 * i, 2)
                return c
            lax.fori_loop(0, units // 2, pair, 0)
            pl.when(units % 2 == 1)(lambda: piece(units - 1, 1))
        by_spans(e, run)
        return carry

    @pl.when(ok_ref[0] != 0)
    def _():
        lax.fori_loop(0, total, tile, 0)

    @pl.when(ok_ref[0] == 0)
    def _():
        half = 128

        def slow_tile(e, carry):
            a = e // tiles
            fetch(e).wait()

            def slow_chunk(i, c):
                rows = pl.ds(pl.multiple_of(i * half, half), half)
                part = acc[a, rows, width:]
                for j in range(frames // half):
                    t = w_buf[e, j * half:(j + 1) * half, :width]
                    inside = lax.broadcasted_iota(jnp.int32, (half, half), 1) + j * half < meta[1, e]
                    sc = nt(s_ref[a, rows, :], t) * scale
                    g = 0.5 * (jnp.exp(jnp.where(inside, sc - row_ref[a, rows, :], -BIG))
                               + jnp.exp(jnp.where(inside, sc - lse_row(e, j), -BIG)))
                    part = part + jnp.dot(g.astype(jnp.bfloat16), t, preferred_element_type=F32)
                acc[a, rows, width:] = part
                return c
            lax.fori_loop(0, ceil_of(meta[3, a], half), slow_chunk, 0)
            return carry
        lax.fori_loop(0, total, slow_tile, 0)

    row = lax.broadcasted_iota(jnp.int32, (frames, width), 0)
    for a in range(2):
        scaled = 0.5 * jnp.exp(-row_ref[a]) * acc[a, :, :width]
        grad = jnp.where(ok_ref[0] != 0, scaled, 0.0) + acc[a, :, width:] - w_buf[a * tiles, :, :width].astype(F32)
        out_ref[a] = jnp.where(row < meta[3, a], grad * scale, 0.0).astype(out_ref.dtype)


def second_pass(tables, ok, student, every, kept, rows, far, own, n_tm, tiles):
    blocks, frames, width = student.shape
    total = blocks * tiles
    smem, vmem, hbm = (pl.BlockSpec(memory_space=m) for m in (pltpu.SMEM, pltpu.VMEM, pl.ANY))
    return pl.pallas_call(
        functools.partial(second_kernel, tiles, n_tm),
        out_shape=jax.ShapeDtypeStruct(student.shape, student.dtype),
        in_specs=[smem, smem, smem, smem, vmem, hbm, hbm, vmem, vmem, vmem],
        out_specs=vmem,
        scratch_shapes=[
            pltpu.VMEM((total, frames, 2 * width), jnp.bfloat16),
            pltpu.VMEM((blocks, frames, 2 * width), F32),
            pltpu.VMEM((total, frames // SPAN, frames, SPAN), jnp.bfloat16),
            pltpu.SMEM((4, total), jnp.int32),
            pltpu.SemaphoreType.DMA((total,)),
            pltpu.SemaphoreType.DMA((total, frames // UNIT)),
        ],
        compiler_params=pltpu.CompilerParams(vmem_limit_bytes=60 * 1024 * 1024),
        name="second_pass",
    )(*tables, ok, student, every, kept, rows, far, own)


def exchange_kernel(n_dp, n_tm, valid_ref, ask_ref, side_ref, send_ref, own_ref, sum_ref, far_ref, lse_ref, loss_ref,
                    inc, reply, across, column, s1, r1, s2, r2, s3, r3, s4, r4):
    me, tm = lax.axis_index("dp"), lax.axis_index("tm")
    others = [(me + o) % n_dp for o in range(1, n_dp)]
    beside = [(tm + o) % n_tm for o in range(1, n_tm)]
    barrier = pltpu.get_barrier_semaphore()
    for to in others:
        pl.semaphore_signal(barrier, inc=1, device_id=(to, tm), device_id_type=MESH)
    for to in beside:
        pl.semaphore_signal(barrier, inc=1, device_id=(me, to), device_id_type=MESH)
    inc[me] = send_ref[me]
    pl.semaphore_wait(barrier, n_dp - 1 + n_tm - 1)

    def ship(src, dst, sent, got, where):
        pltpu.make_async_remote_copy(
            src_ref=src, dst_ref=dst, send_sem=sent, recv_sem=got, device_id=where, device_id_type=MESH).start()

    def settle(buf, sem, count):
        part = buf.at[pl.ds(0, count)]
        pltpu.make_async_copy(part, part, sem).wait()

    for to in others:
        ship(send_ref.at[to], inc.at[me], s1, r1, (to, tm))
    settle(inc, r1, n_dp - 1)
    terms = sum_ref[...] + side_ref[0]
    frame = lax.broadcasted_iota(jnp.int32, (8, 128), 0) * 128 + lax.broadcasted_iota(jnp.int32, (8, 128), 1)
    for a in range(2):
        best = own_ref[a]
        for p in range(n_dp):
            best = jnp.maximum(best, inc[p] + ask_ref[p, a])
        total = jnp.exp(own_ref[a] - best)
        for p in range(n_dp):
            total = total + jnp.exp(inc[p] + ask_ref[p, a] - best)
        lse = jnp.where(frame < valid_ref[(me * n_tm + tm) * 2 + a], best + jnp.log(total), 0.0)
        lse_ref[a] = lse
        terms = terms + lse
    across[tm] = terms
    for p in range(n_dp):
        share = ask_ref[p, 2]
        reply[p] = lse_ref[0] * (1.0 - share) + lse_ref[1] * share
    far_ref[me] = reply[me]
    for to in beside:
        ship(across.at[tm], across.at[tm], s3, r3, (me, to))
    for to in others:
        ship(reply.at[to], far_ref.at[me], s2, r2, (to, tm))
    settle(across, r3, n_tm - 1)
    rows = across[0]
    for t in range(1, n_tm):
        rows = rows + across[t]
    column[me] = rows
    for to in others:
        ship(column.at[me], column.at[me], s4, r4, (to, tm))
    settle(far_ref, r2, n_dp - 1)
    settle(column, r4, n_dp - 1)
    rows = column[0]
    for p in range(1, n_dp):
        rows = rows + column[p]
    loss_ref[...] = jnp.broadcast_to(
        0.5 * jnp.sum(jnp.sum(rows, axis=0, keepdims=True), axis=1, keepdims=True), (8, 128)) / side_ref[1]
    settle(send_ref, s1, n_dp - 1)
    settle(reply, s2, n_dp - 1)
    settle(across, s3, n_tm - 1)
    settle(column, s4, n_dp - 1)


def exchange(valid, ask, side, send, own, sums, n_tm):
    n_dp = send.shape[0]
    smem, vmem = pl.BlockSpec(memory_space=pltpu.SMEM), pl.BlockSpec(memory_space=pltpu.VMEM)
    return pl.pallas_call(
        functools.partial(exchange_kernel, n_dp, n_tm),
        out_shape=(
            jax.ShapeDtypeStruct((n_dp, 8, 128), F32),
            jax.ShapeDtypeStruct((2, 8, 128), F32),
            jax.ShapeDtypeStruct((8, 128), F32),
        ),
        in_specs=[smem] + [vmem] * 5,
        out_specs=(vmem, vmem, vmem),
        scratch_shapes=[
            pltpu.VMEM((n_dp, 8, 128), F32), pltpu.VMEM((n_dp, 8, 128), F32),
            pltpu.VMEM((n_tm, 8, 128), F32), pltpu.VMEM((n_dp, 8, 128), F32),
        ] + [pltpu.SemaphoreType.DMA] * 8,
        compiler_params=pltpu.CompilerParams(collective_id=1, has_side_effects=True),
        name="exchange",
    )(valid, ask, side, send, own, sums)


def body(student, teacher, partner_dp, partner_slot, valid_frames):
    n_dp, n_tm = lax.axis_size("dp"), lax.axis_size("tm")
    blocks, frames, width = student.shape
    tiles = partner_dp.shape[1] + 1
    tables = (partner_dp.T, partner_slot.T, valid_frames)
    every, ask, side = gather(teacher, student, tables, n_dp, n_tm)
    every = every.reshape(n_dp * blocks, frames, width)
    rows, send, own, ok, sums, kept = first_pass(tables, student, every, n_dp, n_tm, tiles)
    far, lse, loss = exchange(valid_frames, ask, side, send, own, sums, n_tm)
    grad = second_pass(tables, ok, student, every, kept, rows, far, lse, n_tm, tiles)
    return (loss[0, 0], grad)


def solution(mesh):
    placed = (P(("dp", "tm"), None, None), P(("dp", "tm"), None, None), P(), P(), P())
    return jax.shard_map(
        body,
        mesh=mesh,
        in_specs=placed,
        out_specs=(P(), P(("dp", "tm"), None, None)),
        check_vma=False,
    )
```

time: 399 us -> 386 us (0.967)
  the two profiles are of different devices: /device:TPU:7 before, /device:TPU:18 now
where the time goes in v2:
time: 386 us
  Pallas kernels  384 us (99%)
    pallas_call x1, Pallas kernels, first_pass(): pl.pallas_call(functools.partial(first_kernel, tiles, n_tm), out_shape=(j...  198 us
    pallas_call x1, Pallas kernels, second_pass(): pl.pallas_call(functools.partial(second_kernel, tiles, n_tm), out_shape=j...  112 us
    pallas_call x1, Pallas kernels, gather(): pl.pallas_call(functools.partial(gather_kernel, rows, n_tm), out_shape=(j...  54.1 us
    pallas_call x1, Pallas kernels, exchange(): pl.pallas_call(functools.partial(exchange_kernel, n_dp, n_tm), out_shape=...  19.2 us

profile of v2, /device:TPU:18, one launch (start us, length us, event | category | flops | bytes accessed | tf_op | source)
XLA Modules:
  0.0 385.8 jit_solution(929177555467952567)
XLA Ops:
  0.6 54.1 %gather.1 = (bf16[32,2,1024,128]{3,2,1,0:T(8,128)(2,1)}, f32[32,3,8,128]{3,2,1,0:T(8,128)}, f32[2,8,128]{2,1,0:T(8,128)}) custom-call(bf16[2,1024,128]{2,1,0:T(8,128)(2,1)} %t_ref.1, bf16[2,1024,128]{2,1,0:T(8,128)(2,1)} %s_ref.5, s32[8,256]{1,0:T(8,128)} %bitcast.6, s32[8,256]{1,0:T(8,128)} %bitcast.9, s32[256]{0:T(256)} %valid_ref.7), custom_call_target="tpu_custom_call" | custom-call | tf_op jit(solution)/shard_map/gather/pallas_call | solution.py:197
  54.7 198.3 %first_pass.1 = (f32[2,1024,128]{2,1,0:T(8,128)}, f32[32,8,128]{2,1,0:T(8,128)}, f32[2,8,128]{2,1,0:T(8,128)}, s32[1]{0:T(128)}, f32[8,128]{1,0:T(8,128)}, /*index=5*/bf16[18,4,1024,256]{3,2,1,0:T(8,128)(2,1)}) custom-call(s32[8,256]{1,0:T(8,128)} %bitcast.7, s32[8,256]{1,0:T(8,128)} %bitcast.10, s32[256]{0:T(256)} %valid_ref.7, ...), custom_call_target="tpu_custom_call" | custom-call | tf_op jit(solution)/shard_map/first_pass/pallas_call | solution.py:408
  253.0 19.2 %exchange.1 = (f32[32,8,128]{2,1,0:T(8,128)}, f32[2,8,128]{2,1,0:T(8,128)}, f32[8,128]{1,0:T(8,128)}) custom-call(s32[256]{0:T(256)} %valid_ref.7, f32[32,3,8,128]{3,2,1,0:T(8,128)} %get-tuple-element.14.ask_ref, f32[2,8,128]{2,1,0:T(8,128)} %get-tuple-element.15.side_ref, f32[32,8,128]{2,1,0:T(8,128)} %get-tuple-element.17.send_ref, ...), custom_call_target="tpu_custom_call" | custom-call | tf_op jit(solution)/shard_map/exchange/pallas_call | solution.py:625
  272.3 112.3 %second_pass.1 = bf16[2,1024,128]{2,1,0:T(8,128)(2,1)} custom-call(s32[8,256]{1,0:T(8,128)} %bitcast.8, s32[8,256]{1,0:T(8,128)} %bitcast.11, s32[256]{0:T(256)} %valid_ref.7, s32[1]{0:T(128)} %get-tuple-element.21.ok_ref, bf16[2,1024,128]{2,1,0:T(8,128)(2,1)} %s_ref.5, bf16[64,1024,128]{2,1,0:T(8,128)(2,1)} %bitcast.5, ...), custom_call_target="tpu_custom_call" | custom-call | tf_op jit(solution)/shard_map/second_pass/pallas_call | solution.py:539
  384.6 1.2 slice.3

commit v3 on v2

--- a/solution.py
+++ b/solution.py
@@ -99,7 +99,12 @@
         total = total + jnp.sum(both.reshape(frames // 8, 8, width), axis=0)
     side_ref[0] = total * (-2.0 / math.sqrt(width))
     count = lax.fori_loop(0, valid_ref.shape[0], lambda i, c: c + valid_ref[i], jnp.int32(0))
-    side_ref[1] = jnp.full((8, width), count).astype(F32)
+    side_ref[1] = 0.5 / jnp.full((8, width), count).astype(F32)
+
+
+def settle(buf, sem, count):
+    part = buf.at[pl.ds(0, count)]
+    pltpu.make_async_copy(part, part, sem).wait()
 
 
 def gather_kernel(rows, n_tm, t_ref, s_ref, dp_ref, slot_ref, valid_ref, out_ref, ask_ref, side_ref,
@@ -122,7 +127,6 @@
     pl.semaphore_wait(barrier, 5)
 
     first, order, _ = plan()
-    sends = []
 
     def recv_id(unit):
         tile, oz, oy, half = unit
@@ -146,22 +150,18 @@
         tile, oz, oy, half = unit
         copy = pltpu.make_async_remote_copy(
             src_ref=source(unit), dst_ref=place(out_ref, unit),
-            send_sem=send_sem.at[len(sends)], recv_sem=recv_sem.at[recv_id((tile, *moved(oz, oy, link), half))],
+            send_sem=send_sem, recv_sem=recv_sem.at[recv_id((tile, *moved(oz, oy, link), half))],
             device_id=(near[link], tm), device_id_type=MESH,
         )
         copy.start()
-        sends.append(copy)
-
-    shares = []
 
     def share(unit):
         copy = pltpu.make_async_remote_copy(
             src_ref=source(unit), dst_ref=place(out_ref, unit),
-            send_sem=peer_send.at[recv_id(unit)], recv_sem=peer_recv.at[recv_id(unit)],
+            send_sem=peer_send, recv_sem=peer_recv,
             device_id=(peer, tm), device_id_type=MESH,
         )
         copy.start()
-        shares.append(copy)
 
     for unit, link in first:
         send(unit, link)
@@ -175,25 +175,21 @@
     for unit, out in order:
         here = place(out_ref, unit)
         pltpu.make_async_remote_copy(
-            src_ref=here, dst_ref=here, send_sem=send_sem.at[0], recv_sem=recv_sem.at[recv_id(unit)],
+            src_ref=here, dst_ref=here, send_sem=send_sem, recv_sem=recv_sem.at[recv_id(unit)],
             device_id=(near[0], tm), device_id_type=MESH,
         ).wait_recv()
         for link in out:
             send(unit, link)
         share(unit)
-    for copy in shares:
-        copy.wait_send()
-        copy.wait_recv()
-    for copy in sends:
-        copy.wait_send()
+    settle(out_ref, peer_send, 16)
+    settle(out_ref, peer_recv, 16)
+    settle(out_ref, send_sem, 15)
     own.wait()
 
 
 def gather(teacher, student, tables, n_dp, n_tm):
     blocks, rows, width = teacher.shape
     smem, vmem, far = (pl.BlockSpec(memory_space=m) for m in (pltpu.SMEM, pltpu.VMEM, pl.ANY))
-    first, order, _ = plan()
-    n_sends = len(first) + sum(len(o) for _, o in order)
     return pl.pallas_call(
         functools.partial(gather_kernel, rows, n_tm),
         out_shape=(
@@ -204,8 +200,8 @@
         in_specs=[vmem, vmem, vmem, vmem, smem],
         out_specs=(far, vmem, vmem),
         scratch_shapes=[
-            pltpu.SemaphoreType.DMA((n_sends,)), pltpu.SemaphoreType.DMA((32 * PARTS,)),
-            pltpu.SemaphoreType.DMA((32 * PARTS,)), pltpu.SemaphoreType.DMA((32 * PARTS,)), pltpu.SemaphoreType.DMA,
+            pltpu.SemaphoreType.DMA, pltpu.SemaphoreType.DMA((32 * PARTS,)),
+            pltpu.SemaphoreType.DMA, pltpu.SemaphoreType.DMA, pltpu.SemaphoreType.DMA,
         ],
         compiler_params=pltpu.CompilerParams(collective_id=0, has_side_effects=True),
         name="gather",
@@ -246,20 +242,31 @@
     return (x + n - 1) // n
 
 
-def stash(e, u, v, inside, outside, sems, out):
-    rows = pl.ds(pl.multiple_of(u * UNIT, UNIT), UNIT)
+def stash(e, v, m, inside, outside, sems, out):
+    rows = pl.ds(0, m * UNIT)
     near, far = inside.at[e, pl.ds(0, v), rows], outside.at[e, pl.ds(0, v), rows]
-    return pltpu.make_async_copy(near, far, sems.at[e, u]) if out else pltpu.make_async_copy(far, near, sems.at[e, u])
+    return pltpu.make_async_copy(near, far, sems.at[e]) if out else pltpu.make_async_copy(far, near, sems.at[e])
+
+
+def by_shape(keys, count, most, run):
+    spans, units = ceil_of(keys, SPAN), ceil_of(count, UNIT)
+    for v in range(1, most + 1):
+        @pl.when(spans == v)
+        def _():
+            for m in range(1, most + 1):
+                pl.when(units == m)(functools.partial(run, v, m))
 
 
 def first_kernel(tiles, n_tm, dp_ref, slot_ref, valid_ref, s_ref, every, row_ref, send_ref, own_ref, ok_ref, sum_ref, e_hbm,
-                 t_buf, right, key_edge, key_full, acc, col, ends, e_buf, meta, sems, e_sems):
+                 s_buf, row_buf, t_buf, right, key_edge, key_full, acc, col, ends, e_buf, meta, sems, e_sems, out_sem):
     me, tm = lax.axis_index("dp"), lax.axis_index("tm")
     frames, width = s_ref.shape[1], s_ref.shape[2]
     total = 2 * tiles
     spans_most = frames // SPAN
     scale = 1.0 / math.sqrt(width)
     c2 = scale / math.log(2.0)
+    bring = pltpu.make_async_copy(s_ref, s_buf, out_sem)
+    bring.start()
     lay_table(meta, tiles, me, tm, n_tm, dp_ref, slot_ref, valid_ref)
 
     def fetch(e):
@@ -289,44 +296,28 @@
             for r in range(8):
                 send_ref[meta[2, e], r:r + 1, :] = values[:, r * 128:(r + 1) * 128]
 
-    def by_spans(e, run):
-        spans = ceil_of(meta[1, e], SPAN)
-        for v in range(1, spans_most + 1):
-            pl.when(spans == v)(functools.partial(run, v))
-
     def tile(e, carry):
         a = e // tiles
         keys = meta[1, e]
         fetch(e).wait()
-        col[...] = jnp.zeros_like(col)
-        units = ceil_of(meta[3, a], UNIT)
         key_edge[...] = edge((SPAN, width), (ceil_of(keys, SPAN) - 1) * SPAN, keys, True)
 
-        def run(v):
-            def piece(u, many):
-                n = UNIT * many
-                rows = pl.ds(pl.multiple_of(u * UNIT, UNIT), n)
-                lhs = jnp.concatenate([s_ref[a, rows, :], right[a, rows, :]], axis=1)
-                part = acc[a, rows, :]
-                for j in range(v):
-                    cols = slice(j * SPAN, (j + 1) * SPAN)
-                    side = key_edge if j == v - 1 else key_full
-                    rhs = jnp.concatenate([t_buf[e, cols, :], side[...]], axis=1)
-                    p = jnp.exp2(nt(lhs, rhs) * c2)
-                    e_buf[e, j, rows, :] = p.astype(jnp.bfloat16)
-                    for w in range(SPAN // 128):
-                        part = part + p[:, w * 128:(w + 1) * 128]
-                    col[:, cols] += jnp.sum(p.reshape(n // 8, 8, SPAN), axis=0)
-                acc[a, rows, :] = part
-                for i in range(many):
-                    stash(e, u + i, v, e_buf, e_hbm, e_sems, True).start()
-
-            def pair(i, c):
-                piece(2 * i, 2)
-                return c
-            lax.fori_loop(0, units // 2, pair, 0)
-            pl.when(units % 2 == 1)(lambda: piece(units - 1, 1))
-        by_spans(e, run)
+        def run(v, m):
+            n = UNIT * m
+            lhs = jnp.concatenate([s_buf[a, :n, :], right[a, :n, :]], axis=1)
+            part = acc[a, :n, :]
+            for j in range(v):
+                cols = slice(j * SPAN, (j + 1) * SPAN)
+                side = key_edge if j == v - 1 else key_full
+                rhs = jnp.concatenate([t_buf[e, cols, :], side[...]], axis=1)
+                p = jnp.exp2(nt(lhs, rhs) * c2)
+                e_buf[e, j, :n, :] = p.astype(jnp.bfloat16)
+                for w in range(SPAN // 128):
+                    part = part + p[:, w * 128:(w + 1) * 128]
+                col[:, cols] = jnp.sum(p.reshape(n // 8, 8, SPAN), axis=0)
+            acc[a, :n, :] = part
+            stash(e, v, m, e_buf, e_hbm, e_sems, True).start()
+        by_shape(keys, meta[3, a], spans_most, run)
         sums = jnp.sum(col[...], axis=0, keepdims=True)
         sums = jnp.where(lane < keys, sums, 1.0)
         ends[0:1, :] = jnp.minimum(ends[0:1, :], sums)
@@ -334,6 +325,7 @@
         put(e, jnp.where(lane < keys, jnp.log(sums), -BIG))
         return carry
 
+    bring.wait()
     lax.fori_loop(0, total, tile, 0)
 
     low, high = jnp.min(ends[0:1, :]), jnp.max(ends[1:2, :])
@@ -342,14 +334,13 @@
         sums = jnp.broadcast_to(jnp.sum(acc[a], axis=1, keepdims=True), (frames, 128))
         sums = jnp.where(row < meta[3, a], sums, 1.0)
         low, high = jnp.minimum(low, jnp.min(sums)), jnp.maximum(high, jnp.max(sums))
-        lse = jnp.log(sums)
-        row_ref[a] = lse
-        sum_ref[...] += jnp.sum(lse.reshape(frames // 8, 8, 128), axis=0)
+        row_buf[a] = (0.5 * scale) / sums
+        sum_ref[...] += jnp.sum(jnp.log(sums).reshape(frames // 8, 8, 128), axis=0)
 
     @pl.when(jnp.logical_not((low >= LOW) & (high <= HIGH)))
     def _():
         ok_ref[0] = 0
-        row_ref[...] = jnp.full(row_ref.shape, -BIG, F32)
+        row_buf[...] = jnp.full(row_buf.shape, -BIG, F32)
         acc[...] = jnp.zeros_like(acc)
         sum_ref[...] = jnp.zeros_like(sum_ref)
         half = 128
@@ -362,16 +353,16 @@
 
             def slow_chunk(i, c):
                 rows = pl.ds(pl.multiple_of(i * half, half), half)
-                lhs = jnp.concatenate([s_ref[a, rows, :], right[a, rows, :]], axis=1)
+                lhs = jnp.concatenate([s_buf[a, rows, :], right[a, rows, :]], axis=1)
                 for j in range(frames // half):
                     cols = slice(j * half, (j + 1) * half)
                     rhs = jnp.concatenate([t_buf[e, cols, :], edge((half, width), j * half, keys, True)], axis=1)
                     sc = nt(lhs, rhs) * scale
-                    old = row_ref[a, rows, :]
+                    old = row_buf[a, rows, :]
                     new = jnp.maximum(old, jnp.broadcast_to(jnp.max(sc, axis=1, keepdims=True), (half, 128)))
                     acc[a, rows, :] = acc[a, rows, :] * jnp.exp(old - new) + jnp.broadcast_to(
                         jnp.sum(jnp.where(sc > -0.01 * BIG, jnp.exp(sc - new[:, :1]), 0.0), axis=1, keepdims=True), (half, 128))
-                    row_ref[a, rows, :] = new
+                    row_buf[a, rows, :] = new
                     cold = col[0:1, cols]
                     cnew = jnp.maximum(cold, jnp.max(sc, axis=0, keepdims=True))
                     col[1:2, cols] = col[1:2, cols] * jnp.exp(cold - cnew) + jnp.sum(
@@ -384,21 +375,20 @@
             return carry
         lax.fori_loop(0, total, slow_tile, 0)
         for a in range(2):
-            lse = jnp.where(row < meta[3, a], row_ref[a] + jnp.log(jnp.maximum(acc[a], 1e-30)), 0.0)
-            row_ref[a] = lse
+            lse = jnp.where(row < meta[3, a], row_buf[a] + jnp.log(jnp.maximum(acc[a], 1e-30)), 0.0)
+            row_buf[a] = lse
             sum_ref[...] += jnp.sum(lse.reshape(frames // 8, 8, 128), axis=0)
 
     sum_ref[...] = sum_ref[...] * (1.0 / 128)
 
+    give = pltpu.make_async_copy(row_buf, row_ref, out_sem)
+    give.start()
+
     def drain(e, carry):
-        def run(v):
-            def one(u, c):
-                stash(e, u, v, e_buf, e_hbm, e_sems, True).wait()
-                return c
-            lax.fori_loop(0, ceil_of(meta[3, e // tiles], UNIT), one, 0)
-        by_spans(e, run)
+        by_shape(meta[1, e], meta[3, e // tiles], spans_most, lambda v, m: stash(e, v, m, e_buf, e_hbm, e_sems, True).wait())
         return carry
     lax.fori_loop(0, total, drain, 0)
+    give.wait()
 
 
 def first_pass(tables, student, every, n_dp, n_tm, tiles):
@@ -415,9 +405,11 @@
             jax.ShapeDtypeStruct((8, 128), F32),
             jax.ShapeDtypeStruct((total, frames // SPAN, frames, SPAN), jnp.bfloat16),
         ),
-        in_specs=[smem, smem, smem, vmem, far],
-        out_specs=(vmem, vmem, vmem, smem, vmem, far),
+        in_specs=[smem, smem, smem, far, far],
+        out_specs=(far, vmem, vmem, smem, vmem, far),
         scratch_shapes=[
+            pltpu.VMEM((blocks, frames, width), jnp.bfloat16),
+            pltpu.VMEM((blocks, frames, 128), F32),
             pltpu.VMEM((total, frames, width), jnp.bfloat16),
             pltpu.VMEM((blocks, frames, width), jnp.bfloat16),
             pltpu.VMEM((SPAN, width), jnp.bfloat16),
@@ -428,7 +420,8 @@
             pltpu.VMEM((total, frames // SPAN, frames, SPAN), jnp.bfloat16),
             pltpu.SMEM((4, total), jnp.int32),
             pltpu.SemaphoreType.DMA((total,)),
-            pltpu.SemaphoreType.DMA((total, frames // UNIT)),
+            pltpu.SemaphoreType.DMA((total,)),
+            pltpu.SemaphoreType.DMA,
         ],
         compiler_params=pltpu.CompilerParams(vmem_limit_bytes=60 * 1024 * 1024),
         name="first_pass",
@@ -436,7 +429,7 @@
 
 
 def second_kernel(tiles, n_tm, dp_ref, slot_ref, valid_ref, ok_ref, s_ref, every, e_hbm, row_ref, far_ref, own_ref, out_ref,
-                  w_buf, acc, e_buf, meta, sems, e_sems):
+                  s_buf, row_buf, w_buf, acc, e_buf, meta, sems, e_sems, row_sem, s_sem):
     me, tm = lax.axis_index("dp"), lax.axis_index("tm")
     frames, width = s_ref.shape[1], s_ref.shape[2]
     total = 2 * tiles
@@ -447,24 +440,17 @@
     def fetch(e):
         return pltpu.make_async_copy(every.at[meta[0, e]], w_buf.at[e, :, pl.ds(0, width)], sems.at[e])
 
-    def by_spans(e, run):
-        spans = ceil_of(meta[1, e], SPAN)
-        for v in range(1, spans_most + 1):
-            pl.when(spans == v)(functools.partial(run, v))
-
     def load(e, carry):
         fetch(e).start()
 
         @pl.when(ok_ref[0] != 0)
         def _():
-            def run(v):
-                def one(u, c):
-                    stash(e, u, v, e_buf, e_hbm, e_sems, False).start()
-                    return c
-                lax.fori_loop(0, ceil_of(meta[3, e // tiles], UNIT), one, 0)
-            by_spans(e, run)
+            by_shape(meta[1, e], meta[3, e // tiles], spans_most,
+                     lambda v, m: stash(e, v, m, e_buf, e_hbm, e_sems, False).start())
         return carry
     lax.fori_loop(0, total, load, 0)
+    rows_in = pltpu.make_async_copy(row_ref, row_buf, row_sem)
+    rows_in.start()
     acc[...] = jnp.zeros_like(acc)
 
     def lse_row(e, r):
@@ -473,28 +459,18 @@
 
     def tile(e, carry):
         a = e // tiles
-        units = ceil_of(meta[3, a], UNIT)
         fetch(e).wait()
 
-        def run(v):
+        def run(v, m):
+            n = UNIT * m
             for r in range(v * SPAN // 128):
                 rows = slice(r * 128, (r + 1) * 128)
-                weight = jnp.broadcast_to(0.5 * jnp.exp(-lse_row(e, r)), (128, 128)).T
+                weight = jnp.broadcast_to((0.5 * scale) * jnp.exp(-lse_row(e, r)), (128, 128)).T
                 w_buf[e, rows, width:] = (weight * w_buf[e, rows, :width].astype(F32)).astype(w_buf.dtype)
-
-            def piece(u, many):
-                for i in range(many):
-                    stash(e, u + i, v, e_buf, e_hbm, e_sems, False).wait()
-                rows = pl.ds(pl.multiple_of(u * UNIT, UNIT), UNIT * many)
-                lhs = jnp.concatenate([e_buf[e, j, rows, :] for j in range(v)], axis=1)
-                acc[a, rows, :] += jnp.dot(lhs, w_buf[e, :v * SPAN, :], preferred_element_type=F32)
-
-            def pair(i, c):
-                piece(2 * i, 2)
-                return c
-            lax.fori_loop(0, units // 2, pair, 0)
-            pl.when(units % 2 == 1)(lambda: piece(units - 1, 1))
-        by_spans(e, run)
+            stash(e, v, m, e_buf, e_hbm, e_sems, False).wait()
+            lhs = jnp.concatenate([e_buf[e, j, :n, :] for j in range(v)], axis=1)
+            acc[a, :n, :] += jnp.dot(lhs, w_buf[e, :v * SPAN, :], preferred_element_type=F32)
+        by_shape(meta[1, e], meta[3, a], spans_most, run)
         return carry
 
     @pl.when(ok_ref[0] != 0)
@@ -504,6 +480,9 @@
     @pl.when(ok_ref[0] == 0)
     def _():
         half = 128
+        students = pltpu.make_async_copy(s_ref, s_buf, s_sem)
+        students.start()
+        students.wait()
 
         def slow_tile(e, carry):
             a = e // tiles
@@ -515,21 +494,22 @@
                 for j in range(frames // half):
                     t = w_buf[e, j * half:(j + 1) * half, :width]
                     inside = lax.broadcasted_iota(jnp.int32, (half, half), 1) + j * half < meta[1, e]
-                    sc = nt(s_ref[a, rows, :], t) * scale
-                    g = 0.5 * (jnp.exp(jnp.where(inside, sc - row_ref[a, rows, :], -BIG))
+                    sc = nt(s_buf[a, rows, :], t) * scale
+                    g = 0.5 * (jnp.exp(jnp.where(inside, sc - row_buf[a, rows, :], -BIG))
                                + jnp.exp(jnp.where(inside, sc - lse_row(e, j), -BIG)))
-                    part = part + jnp.dot(g.astype(jnp.bfloat16), t, preferred_element_type=F32)
+                    part = part + scale * jnp.dot(g.astype(jnp.bfloat16), t, preferred_element_type=F32)
                 acc[a, rows, width:] = part
                 return c
             lax.fori_loop(0, ceil_of(meta[3, a], half), slow_chunk, 0)
             return carry
         lax.fori_loop(0, total, slow_tile, 0)
-
+        acc[:, :, :width] = jnp.zeros_like(acc[:, :, :width])
+
+    rows_in.wait()
     row = lax.broadcasted_iota(jnp.int32, (frames, width), 0)
     for a in range(2):
-        scaled = 0.5 * jnp.exp(-row_ref[a]) * acc[a, :, :width]
-        grad = jnp.where(ok_ref[0] != 0, scaled, 0.0) + acc[a, :, width:] - w_buf[a * tiles, :, :width].astype(F32)
-        out_ref[a] = jnp.where(row < meta[3, a], grad * scale, 0.0).astype(out_ref.dtype)
+        grad = row_buf[a] * acc[a, :, :width] + acc[a, :, width:] - scale * w_buf[a * tiles, :, :width].astype(F32)
+        out_ref[a] = jnp.where(row < meta[3, a], grad, 0.0).astype(out_ref.dtype)
 
 
 def second_pass(tables, ok, student, every, kept, rows, far, own, n_tm, tiles):
@@ -539,15 +519,19 @@
     return pl.pallas_call(
         functools.partial(second_kernel, tiles, n_tm),
         out_shape=jax.ShapeDtypeStruct(student.shape, student.dtype),
-        in_specs=[smem, smem, smem, smem, vmem, hbm, hbm, vmem, vmem, vmem],
+        in_specs=[smem, smem, smem, smem, hbm, hbm, hbm, hbm, vmem, vmem],
         out_specs=vmem,
         scratch_shapes=[
+            pltpu.VMEM((blocks, frames, width), jnp.bfloat16),
+            pltpu.VMEM((blocks, frames, 128), F32),
             pltpu.VMEM((total, frames, 2 * width), jnp.bfloat16),
             pltpu.VMEM((blocks, frames, 2 * width), F32),
             pltpu.VMEM((total, frames // SPAN, frames, SPAN), jnp.bfloat16),
             pltpu.SMEM((4, total), jnp.int32),
             pltpu.SemaphoreType.DMA((total,)),
-            pltpu.SemaphoreType.DMA((total, frames // UNIT)),
+            pltpu.SemaphoreType.DMA((total,)),
+            pltpu.SemaphoreType.DMA,
+            pltpu.SemaphoreType.DMA,
         ],
         compiler_params=pltpu.CompilerParams(vmem_limit_bytes=60 * 1024 * 1024),
         name="second_pass",
@@ -570,10 +554,6 @@
     def ship(src, dst, sent, got, where):
         pltpu.make_async_remote_copy(
             src_ref=src, dst_ref=dst, send_sem=sent, recv_sem=got, device_id=where, device_id_type=MESH).start()
-
-    def settle(buf, sem, count):
-        part = buf.at[pl.ds(0, count)]
-        pltpu.make_async_copy(part, part, sem).wait()
 
     for to in others:
         ship(send_ref.at[to], inc.at[me], s1, r1, (to, tm))
@@ -611,8 +591,7 @@
     rows = column[0]
     for p in range(1, n_dp):
         rows = rows + column[p]
-    loss_ref[...] = jnp.broadcast_to(
-        0.5 * jnp.sum(jnp.sum(rows, axis=0, keepdims=True), axis=1, keepdims=True), (8, 128)) / side_ref[1]
+    loss_ref[0] = jnp.sum(rows * side_ref[1])
     settle(send_ref, s1, n_dp - 1)
     settle(reply, s2, n_dp - 1)
     settle(across, s3, n_tm - 1)
@@ -627,10 +606,10 @@
         out_shape=(
             jax.ShapeDtypeStruct((n_dp, 8, 128), F32),
             jax.ShapeDtypeStruct((2, 8, 128), F32),
-            jax.ShapeDtypeStruct((8, 128), F32),
+            jax.ShapeDtypeStruct((1,), F32),
         ),
         in_specs=[smem] + [vmem] * 5,
-        out_specs=(vmem, vmem, vmem),
+        out_specs=(vmem, vmem, smem),
         scratch_shapes=[
             pltpu.VMEM((n_dp, 8, 128), F32), pltpu.VMEM((n_dp, 8, 128), F32),
             pltpu.VMEM((n_tm, 8, 128), F32), pltpu.VMEM((n_dp, 8, 128), F32),
@@ -650,7 +629,7 @@
     rows, send, own, ok, sums, kept = first_pass(tables, student, every, n_dp, n_tm, tiles)
     far, lse, loss = exchange(valid_frames, ask, side, send, own, sums, n_tm)
     grad = second_pass(tables, ok, student, every, kept, rows, far, lse, n_tm, tiles)
-    return (loss[0, 0], grad)
+    return (loss[0], grad)
 
 
 def solution(mesh):

time: 386 us -> 491 us (1.27)
  Pallas kernels: 384 us -> 489 us
    pallas_call x1, Pallas kernels: 112 us -> 222 us  [second_pass(): pl.pallas_call(functools.partial(second_kernel, tiles, n_tm), out_shape=j...]
where the time goes in v3:
time: 491 us
  Pallas kernels  489 us (100%)
    pallas_call x1, Pallas kernels, second_pass(): pl.pallas_call(functools.partial(second_kernel, tiles, n_tm), out_shape=j...  222 us
    pallas_call x1, Pallas kernels, first_pass(): pl.pallas_call(functools.partial(first_kernel, tiles, n_tm), out_shape=(j...  195 us
    pallas_call x1, Pallas kernels, gather(): pl.pallas_call(functools.partial(gather_kernel, rows, n_tm), out_shape=(j...  52.4 us
    pallas_call x1, Pallas kernels, exchange(): pl.pallas_call(functools.partial(exchange_kernel, n_dp, n_tm), out_shape=...  19.3 us

profile of v3, /device:TPU:18, one launch (start us, length us, event | category | flops | bytes accessed | tf_op | source)
XLA Modules:
  0.0 491.1 jit_solution(6311734366283678377)
XLA Ops:
  0.6 52.4 %gather.1 = (bf16[32,2,1024,128]{3,2,1,0:T(8,128)(2,1)}, f32[32,3,8,128]{3,2,1,0:T(8,128)}, f32[2,8,128]{2,1,0:T(8,128)}) custom-call(bf16[2,1024,128]{2,1,0:T(8,128)(2,1)} %t_ref.1, bf16[2,1024,128]{2,1,0:T(8,128)(2,1)} %s_ref.5, s32[8,256]{1,0:T(8,128)} %bitcast.6, s32[8,256]{1,0:T(8,128)} %bitcast.9, s32[256]{0:T(256)} %valid_ref.7), custom_call_target="tpu_custom_call" | custom-call | tf_op jit(solution)/shard_map/gather/pallas_call | solution.py:193
  53.0 194.7 %first_pass.1 = (f32[2,1024,128]{2,1,0:T(8,128)}, f32[32,8,128]{2,1,0:T(8,128)}, f32[2,8,128]{2,1,0:T(8,128)}, s32[1]{0:T(128)}, f32[8,128]{1,0:T(8,128)}, /*index=5*/bf16[18,4,1024,256]{3,2,1,0:T(8,128)(2,1)}) custom-call(s32[8,256]{1,0:T(8,128)} %bitcast.7, s32[8,256]{1,0:T(8,128)} %bitcast.10, s32[256]{0:T(256)} %valid_ref.7, ...), custom_call_target="tpu_custom_call" | custom-call | tf_op jit(solution)/shard_map/first_pass/pallas_call | solution.py:398
  247.7 19.3 %exchange.1 = (f32[32,8,128]{2,1,0:T(8,128)}, f32[2,8,128]{2,1,0:T(8,128)}, f32[1]{0:T(128)}) custom-call(s32[256]{0:T(256)} %valid_ref.7, f32[32,3,8,128]{3,2,1,0:T(8,128)} %get-tuple-element.14.ask_ref, f32[2,8,128]{2,1,0:T(8,128)} %get-tuple-element.15.side_ref, f32[32,8,128]{2,1,0:T(8,128)} %get-tuple-element.17.send_ref, ...), custom_call_target="tpu_custom_call" | custom-call | tf_op jit(solution)/shard_map/exchange/pallas_call | solution.py:604
  267.0 222.4 %second_pass.1 = bf16[2,1024,128]{2,1,0:T(8,128)(2,1)} custom-call(s32[8,256]{1,0:T(8,128)} %bitcast.8, s32[8,256]{1,0:T(8,128)} %bitcast.11, s32[256]{0:T(256)} %valid_ref.7, s32[1]{0:T(128)} %get-tuple-element.21.ok_ref, bf16[2,1024,128]{2,1,0:T(8,128)(2,1)} %s_ref.5, bf16[64,1024,128]{2,1,0:T(8,128)(2,1)} %bitcast.5, ...), custom_call_target="tpu_custom_call" | custom-call | tf_op jit(solution)/shard_map/second_pass/pallas_call | solution.py:519

commit v4 on v3

--- a/solution.py
+++ b/solution.py
@@ -13,11 +13,16 @@
 F32 = jnp.float32
 BIG = 1e30
 
+PARTS = 2
 ZP, ZM, YP, YM = range(4)
 MOVE = {ZP: (1, 0), ZM: (-1, 0), YP: (0, 1), YM: (0, -1)}
-
-
-PARTS = 2
+FIRST = ((0, 0), (0, 1), (0, 3), (1, 0), (3, 0), (2, 0), (1, 1), (3, 1), (0, 2), (1, 3), (3, 3))
+NEXT = ((2, 1), (2, 3))
+LAST = ((1, 2), (3, 2), (2, 2))
+CHIPS = FIRST + NEXT + LAST
+EARLY = 10
+SURE = 6
+STARTED = 2 + EARLY
 
 
 def onward(tile, oz, oy, part):
@@ -52,11 +57,10 @@
 
     def send(unit, link, now):
         nonlocal count
-        tile, oz, oy, half = unit
-        start = max(now, free[link])
-        free[link] = start + 1.0
+        tile, oz, oy, part = unit
+        free[link] = max(now, free[link]) + 1.0
         noz, noy = moved(oz, oy, link)
-        heapq.heappush(events, (free[link] + 0.5, count, (tile, noz, noy, half), link))
+        heapq.heappush(events, (free[link] + 0.5, count, (tile, noz, noy, part), link))
         count += 1
 
     first = []
@@ -75,7 +79,7 @@
         order.append((unit, out))
         for link in out:
             send(unit, link, now)
-    return first, order, max(free)
+    return first, order
 
 
 def lay_requests(me, tm, n_tm, dp_ref, slot_ref, ask_ref):
@@ -107,14 +111,21 @@
     pltpu.make_async_copy(part, part, sem).wait()
 
 
-def gather_kernel(rows, n_tm, t_ref, s_ref, dp_ref, slot_ref, valid_ref, out_ref, ask_ref, side_ref,
-                  send_sem, recv_sem, peer_send, peer_recv, own_sem):
-    half_rows = rows // PARTS
+def gather_kernel(n_tm, t_ref, s_ref, dpv_ref, slotv_ref, dp_ref, slot_ref, valid_ref,
+                  out_ref, e_hbm, acc_hbm, ask_hbm, side_ref, order_ref, col_ref,
+                  first_buf, next_buf, e_buf, acc, right, ask, found_at, rank_at,
+                  send_sem, recv_sem, peer_send, peer_recv, own_sem, out_sem, e_sem, more_sem):
+    frames, width = t_ref.shape[1], t_ref.shape[2]
+    n = frames // PARTS
     me, tm = lax.axis_index("dp"), lax.axis_index("tm")
     z, y, c = me // 8, (me // 2) % 4, me % 2
+    c2 = 1.0 / math.sqrt(width) / math.log(2.0)
 
     def dp_of(zz, yy, cc):
         return (zz * 4 + yy) * 2 + cc
+
+    def device_of(oz, oy, cc):
+        return dp_of((z + 4 - oz) % 4, (y + 4 - oy) % 4, cc)
 
     near = [
         dp_of((z + 1) % 4, y, c), dp_of((z + 3) % 4, y, c),
@@ -126,54 +137,142 @@
         pl.semaphore_signal(barrier, inc=1, device_id=(other, tm), device_id_type=MESH)
     pl.semaphore_wait(barrier, 5)
 
-    first, order, _ = plan()
-
     def recv_id(unit):
-        tile, oz, oy, half = unit
-        return ((tile * 4 + oz) * 4 + oy) * PARTS + half
-
-    def slot(unit):
-        _, oz, oy, _ = unit
-        return dp_of((z + 4 - oz) % 4, (y + 4 - oy) % 4, c)
-
-    def place(ref, unit):
-        tile, oz, oy, half = unit
-        return ref.at[slot(unit), tile, pl.ds(half * half_rows, half_rows)]
+        tile, oz, oy, part = unit
+        return ((tile * 4 + oz) * 4 + oy) * PARTS + part
+
+    def device_store(oz, oy, cc):
+        if (oz, oy) in FIRST:
+            return first_buf.at[FIRST.index((oz, oy)) * 2 + cc]
+        if (oz, oy) in NEXT:
+            return next_buf.at[NEXT.index((oz, oy)) * 2 + cc]
+        return out_ref.at[device_of(oz, oy, cc)]
+
+    def place(unit):
+        tile, oz, oy, part = unit
+        return device_store(oz, oy, c).at[tile, pl.ds(part * n, n)]
 
     def source(unit):
-        tile, oz, oy, half = unit
-        if oz == 0 and oy == 0:
-            return t_ref.at[tile, pl.ds(half * half_rows, half_rows)]
-        return place(out_ref, unit)
+        tile, oz, oy, part = unit
+        return t_ref.at[tile, pl.ds(part * n, n)] if (oz, oy) == (0, 0) else place(unit)
+
+    def onto(unit, link):
+        tile, oz, oy, part = unit
+        noz, noy = moved(oz, oy, link)
+        if (noz, noy) in LAST:
+            return out_ref.at[device_of(oz, oy, c), tile, pl.ds(part * n, n)]
+        return place((tile, noz, noy, part))
 
     def send(unit, link):
-        tile, oz, oy, half = unit
-        copy = pltpu.make_async_remote_copy(
-            src_ref=source(unit), dst_ref=place(out_ref, unit),
-            send_sem=send_sem, recv_sem=recv_sem.at[recv_id((tile, *moved(oz, oy, link), half))],
+        tile, oz, oy, part = unit
+        pltpu.make_async_remote_copy(
+            src_ref=source(unit), dst_ref=onto(unit, link),
+            send_sem=send_sem, recv_sem=recv_sem.at[recv_id((tile, *moved(oz, oy, link), part))],
             device_id=(near[link], tm), device_id_type=MESH,
-        )
-        copy.start()
+        ).start()
+
+    def group(oz, oy):
+        return 0 if (oz, oy) in FIRST else 1 if (oz, oy) in NEXT else 2
 
     def share(unit):
-        copy = pltpu.make_async_remote_copy(
-            src_ref=source(unit), dst_ref=place(out_ref, unit),
-            send_sem=peer_send, recv_sem=peer_recv,
+        pltpu.make_async_remote_copy(
+            src_ref=source(unit), dst_ref=place(unit),
+            send_sem=peer_send, recv_sem=peer_recv.at[group(unit[1], unit[2])],
             device_id=(peer, tm), device_id_type=MESH,
-        )
-        copy.start()
-
+        ).start()
+
+    def keep(oz, oy, cc):
+        pltpu.make_async_copy(device_store(oz, oy, cc), out_ref.at[device_of(oz, oy, cc)], out_sem).start()
+
+    first, order = plan()
     for unit, link in first:
         send(unit, link)
     for tile in (0, 1):
-        for half in range(PARTS):
-            share((tile, 0, 0, half))
-    own = pltpu.make_async_copy(t_ref, out_ref.at[me], own_sem)
+        for part in range(PARTS):
+            share((tile, 0, 0, part))
+    own = pltpu.make_async_copy(t_ref, device_store(0, 0, c), own_sem)
     own.start()
-    lay_requests(me, tm, n_tm, dp_ref, slot_ref, ask_ref)
-    lay_side(me, tm, n_tm, t_ref, s_ref, valid_ref, side_ref)
-    for unit, out in order:
-        here = place(out_ref, unit)
+    pltpu.make_async_copy(t_ref, out_ref.at[me], out_sem).start()
+
+    mine = (me * n_tm + tm) * 2
+    partners = dp_ref.shape[0]
+
+    def lay_order():
+        names = [dp_ref[k, mine + a] for a in range(2) for k in range(partners)]
+        rank = jnp.int32(0)
+        for q in range(2 * len(CHIPS)):
+            p = device_of(*CHIPS[q // 2], q % 2)
+            found = jnp.int32(0)
+            for j, name in enumerate(names):
+                found = jnp.where(name == p, j + 1, found)
+            found_at[q] = found
+            rank_at[q] = jnp.where(found > 0, rank, -1)
+            rank = rank + jnp.where(found > 0, 1, 0)
+        where_ = []
+        for r in range(2 * partners):
+            at, entry = jnp.int32(0), jnp.int32(0)
+            for q in range(r, r + 2 * partners + 1):
+                if q < 2 * len(CHIPS):
+                    hit = rank_at[q] == r
+                    at = jnp.where(hit, q, at)
+                    entry = jnp.where(hit, found_at[q] - 1, entry)
+            order_ref[r] = entry
+            where_.append(at)
+        return where_
+
+    def score(pos, a, keys, load, own_block):
+        lhs = jnp.concatenate([s_ref[a], right[a]], axis=1)
+        part = jnp.zeros((frames, 128), F32)
+        for j in range(frames // SPAN):
+            rhs = jnp.concatenate([load(slice(j * SPAN, (j + 1) * SPAN)), edge((SPAN, width), j * SPAN, keys, True)], axis=1)
+            p = jnp.exp2(nt(lhs, rhs) * c2)
+            e_buf[pos, j] = p.astype(jnp.bfloat16)
+            for w in range(SPAN // 128):
+                part = part + p[:, w * 128:(w + 1) * 128]
+            sums = jnp.sum(p, axis=0, keepdims=True)
+            for w in range(SPAN // 128):
+                r = j * (SPAN // 128) + w
+                col_ref[pos, r:r + 1, :] = sums[:, w * 128:(w + 1) * 128]
+        if own_block:
+            acc[a] = part
+        else:
+            for b in range(2):
+                acc[b] += jnp.where(a == b, part, 0.0)
+        pltpu.make_async_copy(e_buf.at[pos], e_hbm.at[pos], e_sem).start()
+
+    def score_own(a):
+        score(a, a, valid_ref[mine + a], lambda rows: t_ref[a, rows, :], True)
+
+    def score_early(r, at):
+        entry = order_ref[r]
+        a, k = entry // partners, entry % partners
+        slot = slot_ref[k, mine + a]
+        keys = valid_ref[(dp_ref[k, mine + a] * n_tm + tm) * 2 + slot]
+        many = 2 * len(FIRST)
+
+        def load(rows):
+            block = first_buf[jnp.minimum(at, many - 1), slot, rows, :]
+            if r < SURE:
+                return block
+            later = next_buf[jnp.clip(at - many, 0, 2 * len(NEXT) - 1), slot, rows, :]
+            return jnp.where(at < many, block, later)
+        score(2 + r, a, keys, load, False)
+
+    right[0] = edge((frames, width), 0, valid_ref[mine], False)
+    right[1] = edge((frames, width), 0, valid_ref[mine + 1], False)
+    lay_requests(me, tm, n_tm, dpv_ref, slotv_ref, ask)
+    asks = pltpu.make_async_copy(ask, ask_hbm, more_sem.at[0])
+    asks.start()
+    at = lay_order()
+    spots = [unit[1:3] for unit, _ in order]
+    first_done = max(i for i, s in enumerate(spots) if s in FIRST)
+    next_done = max(i for i, s in enumerate(spots) if s in NEXT)
+    work = {4: lambda: lay_side(me, tm, n_tm, t_ref, s_ref, valid_ref, side_ref),
+            6: lambda: score_own(0), 12: lambda: score_own(1)}
+    missing = {chip: 2 * PARTS for chip in CHIPS}
+    waiting = []
+    for i, (unit, out) in enumerate(order):
+        here = place(unit)
         pltpu.make_async_remote_copy(
             src_ref=here, dst_ref=here, send_sem=send_sem, recv_sem=recv_sem.at[recv_id(unit)],
             device_id=(near[0], tm), device_id_type=MESH,
@@ -181,31 +280,72 @@
         for link in out:
             send(unit, link)
         share(unit)
-    settle(out_ref, peer_send, 16)
-    settle(out_ref, peer_recv, 16)
-    settle(out_ref, send_sem, 15)
-    own.wait()
+        chip = unit[1:3]
+        missing[chip] -= 1
+        if missing[chip] == 0 and chip not in LAST:
+            keep(*chip, c)
+        if i in work:
+            work[i]()
+        if i == first_done + 1:
+            own.wait()
+            settle(first_buf, peer_recv.at[0], len(FIRST))
+            for chip in FIRST:
+                keep(*chip, 1 - c)
+            waiting += list(range(SURE))
+        if i == next_done + 1:
+            settle(next_buf, peer_recv.at[1], len(NEXT))
+            for chip in NEXT:
+                keep(*chip, 1 - c)
+            waiting += list(range(SURE, EARLY))
+        if waiting:
+            r = waiting.pop(0)
+            score_early(r, at[r])
+    for r in waiting:
+        score_early(r, at[r])
+    sums = pltpu.make_async_copy(acc, acc_hbm, more_sem.at[1])
+    sums.start()
+    settle(out_ref, peer_recv.at[2], len(LAST))
+    settle(out_ref, peer_send, len(CHIPS))
+    settle(out_ref, send_sem, len(CHIPS) - 1)
+    settle(out_ref, out_sem, 2 * (len(FIRST) + len(NEXT)))
+    settle(e_hbm, e_sem, STARTED)
+    asks.wait()
+    sums.wait()
 
 
 def gather(teacher, student, tables, n_dp, n_tm):
-    blocks, rows, width = teacher.shape
+    blocks, frames, width = teacher.shape
     smem, vmem, far = (pl.BlockSpec(memory_space=m) for m in (pltpu.SMEM, pltpu.VMEM, pl.ANY))
+    kept = (STARTED, frames // SPAN, frames, SPAN)
+    dma = pltpu.SemaphoreType.DMA
     return pl.pallas_call(
-        functools.partial(gather_kernel, rows, n_tm),
+        functools.partial(gather_kernel, n_tm),
         out_shape=(
-            jax.ShapeDtypeStruct((n_dp, blocks, rows, width), teacher.dtype),
+            jax.ShapeDtypeStruct((n_dp, blocks, frames, width), teacher.dtype),
+            jax.ShapeDtypeStruct(kept, jnp.bfloat16),
+            jax.ShapeDtypeStruct((blocks, frames, 128), F32),
             jax.ShapeDtypeStruct((n_dp, 3, 8, 128), F32),
             jax.ShapeDtypeStruct((2, 8, 128), F32),
+            jax.ShapeDtypeStruct((blocks * tables[0].shape[0],), jnp.int32),
+            jax.ShapeDtypeStruct((STARTED, 8, 128), F32),
         ),
-        in_specs=[vmem, vmem, vmem, vmem, smem],
-        out_specs=(far, vmem, vmem),
+        in_specs=[vmem, vmem, vmem, vmem, smem, smem, smem],
+        out_specs=(far, far, far, far, vmem, smem, vmem),
         scratch_shapes=[
-            pltpu.SemaphoreType.DMA, pltpu.SemaphoreType.DMA((32 * PARTS,)),
-            pltpu.SemaphoreType.DMA, pltpu.SemaphoreType.DMA, pltpu.SemaphoreType.DMA,
+            pltpu.VMEM((2 * len(FIRST), blocks, frames, width), teacher.dtype),
+            pltpu.VMEM((2 * len(NEXT), blocks, frames, width), teacher.dtype),
+            pltpu.VMEM(kept, jnp.bfloat16),
+            pltpu.VMEM((blocks, frames, 128), F32),
+            pltpu.VMEM((blocks, frames, width), jnp.bfloat16),
+            pltpu.VMEM((n_dp, 3, 8, 128), F32),
+            pltpu.SMEM((2 * len(CHIPS),), jnp.int32),
+            pltpu.SMEM((2 * len(CHIPS),), jnp.int32),
+            dma, dma((32 * PARTS,)), dma, dma((3,)), dma, dma, dma, dma((2,)),
         ],
-        compiler_params=pltpu.CompilerParams(collective_id=0, has_side_effects=True),
+        compiler_params=pltpu.CompilerParams(
+            collective_id=0, has_side_effects=True, vmem_limit_bytes=60 * 1024 * 1024),
         name="gather",
-    )(teacher, student, *tables)
+    )(teacher, student, tables[0], tables[1], *tables)
 
 
 LOW, HIGH = 2.0 ** -60, 2.0 ** 100
@@ -213,18 +353,20 @@
 UNIT = 256
 
 
-def lay_table(meta, tiles, me, tm, n_tm, dp_ref, slot_ref, valid_ref):
-    for a in range(2):
-        mine = (me * n_tm + tm) * 2 + a
-        meta[3, a] = valid_ref[mine]
-        meta[0, a * tiles] = me * 2 + a
-        meta[1, a * tiles] = valid_ref[mine]
-        meta[2, a * tiles] = 0
-        for k in range(1, tiles):
-            far, slot = dp_ref[k - 1, mine], slot_ref[k - 1, mine]
-            meta[0, a * tiles + k] = far * 2 + slot
-            meta[1, a * tiles + k] = valid_ref[(far * n_tm + tm) * 2 + slot]
-            meta[2, a * tiles + k] = far
+def lay_table(meta, tiles, me, tm, n_tm, dp_ref, slot_ref, valid_ref, order_ref):
+    mine = (me * n_tm + tm) * 2
+    for e in range(2 * tiles):
+        if e < 2:
+            a, far, slot = e, me, e
+        else:
+            entry = order_ref[e - 2]
+            a, k = entry // (tiles - 1), entry % (tiles - 1)
+            far, slot = dp_ref[k, mine + a], slot_ref[k, mine + a]
+        meta[0, e] = far * 2 + slot
+        meta[1, e] = valid_ref[(far * n_tm + tm) * 2 + slot]
+        meta[2, e] = far
+        meta[3, e] = a
+        meta[4, e] = valid_ref[mine + a]
 
 
 def edge(shape, start, count, key):
@@ -242,9 +384,9 @@
     return (x + n - 1) // n
 
 
-def stash(e, v, m, inside, outside, sems, out):
+def stash(e, v, m, inside, outside, sems, out, skip=0):
     rows = pl.ds(0, m * UNIT)
-    near, far = inside.at[e, pl.ds(0, v), rows], outside.at[e, pl.ds(0, v), rows]
+    near, far = inside.at[e, pl.ds(0, v), rows], outside.at[e - skip, pl.ds(0, v), rows]
     return pltpu.make_async_copy(near, far, sems.at[e]) if out else pltpu.make_async_copy(far, near, sems.at[e])
 
 
@@ -257,8 +399,8 @@
                 pl.when(units == m)(functools.partial(run, v, m))
 
 
-def first_kernel(tiles, n_tm, dp_ref, slot_ref, valid_ref, s_ref, every, row_ref, send_ref, own_ref, ok_ref, sum_ref, e_hbm,
-                 s_buf, row_buf, t_buf, right, key_edge, key_full, acc, col, ends, e_buf, meta, sems, e_sems, out_sem):
+def first_kernel(tiles, n_tm, dp_ref, slot_ref, valid_ref, order_ref, s_ref, every, sofar_ref, col_ref, row_ref, send_ref, own_ref, ok_ref, sum_ref, e_hbm,
+                 s_buf, row_buf, t_buf, right, key_edge, key_full, acc, col, ends, e_buf, meta, sems, e_sems, out_sem, row_sem):
     me, tm = lax.axis_index("dp"), lax.axis_index("tm")
     frames, width = s_ref.shape[1], s_ref.shape[2]
     total = 2 * tiles
@@ -267,16 +409,15 @@
     c2 = scale / math.log(2.0)
     bring = pltpu.make_async_copy(s_ref, s_buf, out_sem)
     bring.start()
-    lay_table(meta, tiles, me, tm, n_tm, dp_ref, slot_ref, valid_ref)
+    lay_table(meta, tiles, me, tm, n_tm, dp_ref, slot_ref, valid_ref, order_ref)
 
     def fetch(e):
         return pltpu.make_async_copy(every.at[meta[0, e]], t_buf.at[e], sems.at[e])
-    for e in range(total):
+    for e in range(STARTED, total):
         fetch(e).start()
     for a in range(2):
-        right[a] = edge((frames, width), 0, meta[3, a], False)
+        right[a] = edge((frames, width), 0, meta[4, a], False)
     key_full[...] = edge((SPAN, width), 0, SPAN, True)
-    acc[...] = jnp.zeros_like(acc)
     ok_ref[0] = 1
     sum_ref[...] = jnp.zeros_like(sum_ref)
     ends[...] = jnp.ones_like(ends)
@@ -284,20 +425,28 @@
     send_ref[...] = jnp.zeros_like(send_ref)
 
     def put(e, values):
-        a, k = e // tiles, e % tiles
-
-        @pl.when(k == 0)
+        @pl.when(e < 2)
         def _():
-            for r in range(8):
-                own_ref[a, r:r + 1, :] = values[:, r * 128:(r + 1) * 128]
-
-        @pl.when(k != 0)
+            own_ref[e] = values
+
+        @pl.when(e >= 2)
         def _():
-            for r in range(8):
-                send_ref[meta[2, e], r:r + 1, :] = values[:, r * 128:(r + 1) * 128]
+            send_ref[meta[2, e]] = values
+
+    def fold(sums):
+        return jnp.concatenate([sums[:, r * 128:(r + 1) * 128] for r in range(frames // 128)], axis=0)
+
+    frame = lax.broadcasted_iota(jnp.int32, (8, 128), 0) * 128 + lax.broadcasted_iota(jnp.int32, (8, 128), 1)
+
+    def finish(e, sums):
+        real = frame < meta[1, e]
+        sums = jnp.where(real, sums, 1.0)
+        ends[0] = jnp.minimum(ends[0], sums)
+        ends[1] = jnp.maximum(ends[1], sums)
+        put(e, jnp.where(real, jnp.log(sums), -BIG))
 
     def tile(e, carry):
-        a = e // tiles
+        a = meta[3, e]
         keys = meta[1, e]
         fetch(e).wait()
         key_edge[...] = edge((SPAN, width), (ceil_of(keys, SPAN) - 1) * SPAN, keys, True)
@@ -311,28 +460,29 @@
                 side = key_edge if j == v - 1 else key_full
                 rhs = jnp.concatenate([t_buf[e, cols, :], side[...]], axis=1)
                 p = jnp.exp2(nt(lhs, rhs) * c2)
-                e_buf[e, j, :n, :] = p.astype(jnp.bfloat16)
+                e_buf[e - STARTED, j, :n, :] = p.astype(jnp.bfloat16)
                 for w in range(SPAN // 128):
                     part = part + p[:, w * 128:(w + 1) * 128]
                 col[:, cols] = jnp.sum(p.reshape(n // 8, 8, SPAN), axis=0)
             acc[a, :n, :] = part
-            stash(e, v, m, e_buf, e_hbm, e_sems, True).start()
-        by_shape(keys, meta[3, a], spans_most, run)
-        sums = jnp.sum(col[...], axis=0, keepdims=True)
-        sums = jnp.where(lane < keys, sums, 1.0)
-        ends[0:1, :] = jnp.minimum(ends[0:1, :], sums)
-        ends[1:2, :] = jnp.maximum(ends[1:2, :], sums)
-        put(e, jnp.where(lane < keys, jnp.log(sums), -BIG))
+            stash(e - STARTED, v, m, e_buf, e_hbm, e_sems, True).start()
+        by_shape(keys, meta[4, e], spans_most, run)
+        finish(e, fold(jnp.sum(col[...], axis=0, keepdims=True)))
         return carry
 
+    sofar = pltpu.make_async_copy(sofar_ref, acc, row_sem)
+    sofar.start()
+    for e in range(STARTED):
+        finish(e, col_ref[e])
+    sofar.wait()
     bring.wait()
-    lax.fori_loop(0, total, tile, 0)
-
-    low, high = jnp.min(ends[0:1, :]), jnp.max(ends[1:2, :])
+    lax.fori_loop(STARTED, total, tile, 0)
+
+    low, high = jnp.min(ends[0]), jnp.max(ends[1])
     row = lax.broadcasted_iota(jnp.int32, (frames, 128), 0)
     for a in range(2):
         sums = jnp.broadcast_to(jnp.sum(acc[a], axis=1, keepdims=True), (frames, 128))
-        sums = jnp.where(row < meta[3, a], sums, 1.0)
+        sums = jnp.where(row < meta[4, a], sums, 1.0)
         low, high = jnp.minimum(low, jnp.min(sums)), jnp.maximum(high, jnp.max(sums))
         row_buf[a] = (0.5 * scale) / sums
         sum_ref[...] += jnp.sum(jnp.log(sums).reshape(frames // 8, 8, 128), axis=0)
@@ -344,9 +494,13 @@
         acc[...] = jnp.zeros_like(acc)
         sum_ref[...] = jnp.zeros_like(sum_ref)
         half = 128
+        for e in range(STARTED):
+            fetch(e).start()
+        for e in range(STARTED):
+            fetch(e).wait()
 
         def slow_tile(e, carry):
-            a = e // tiles
+            a = meta[3, e]
             keys = meta[1, e]
             col[0:1, :] = jnp.full((1, frames), -BIG, F32)
             col[1:2, :] = jnp.zeros((1, frames), F32)
@@ -371,11 +525,11 @@
                 return c
             lax.fori_loop(0, frames // half, slow_chunk, 0)
             real = lane < keys
-            put(e, jnp.where(real, col[0:1, :] + jnp.log(jnp.where(real, col[1:2, :], 1.0)), -BIG))
+            put(e, fold(jnp.where(real, col[0:1, :] + jnp.log(jnp.where(real, col[1:2, :], 1.0)), -BIG)))
             return carry
         lax.fori_loop(0, total, slow_tile, 0)
         for a in range(2):
-            lse = jnp.where(row < meta[3, a], row_buf[a] + jnp.log(jnp.maximum(acc[a], 1e-30)), 0.0)
+            lse = jnp.where(row < meta[4, a], row_buf[a] + jnp.log(jnp.maximum(acc[a], 1e-30)), 0.0)
             row_buf[a] = lse
             sum_ref[...] += jnp.sum(lse.reshape(frames // 8, 8, 128), axis=0)
 
@@ -385,13 +539,13 @@
     give.start()
 
     def drain(e, carry):
-        by_shape(meta[1, e], meta[3, e // tiles], spans_most, lambda v, m: stash(e, v, m, e_buf, e_hbm, e_sems, True).wait())
+        by_shape(meta[1, e], meta[4, e], spans_most, lambda v, m: stash(e - STARTED, v, m, e_buf, e_hbm, e_sems, True).wait())
         return carry
-    lax.fori_loop(0, total, drain, 0)
+    lax.fori_loop(STARTED, total, drain, 0)
     give.wait()
 
 
-def first_pass(tables, student, every, n_dp, n_tm, tiles):
+def first_pass(tables, student, every, sofar, cols, n_dp, n_tm, tiles):
     blocks, frames, width = student.shape
     total = blocks * tiles
     smem, vmem, far = (pl.BlockSpec(memory_space=m) for m in (pltpu.SMEM, pltpu.VMEM, pl.ANY))
@@ -403,9 +557,9 @@
             jax.ShapeDtypeStruct((blocks, 8, 128), F32),
             jax.ShapeDtypeStruct((1,), jnp.int32),
             jax.ShapeDtypeStruct((8, 128), F32),
-            jax.ShapeDtypeStruct((total, frames // SPAN, frames, SPAN), jnp.bfloat16),
+            jax.ShapeDtypeStruct((total - STARTED, frames // SPAN, frames, SPAN), jnp.bfloat16),
         ),
-        in_specs=[smem, smem, smem, far, far],
+        in_specs=[smem, smem, smem, smem, far, far, far, vmem],
         out_specs=(far, vmem, vmem, smem, vmem, far),
         scratch_shapes=[
             pltpu.VMEM((blocks, frames, width), jnp.bfloat16),
@@ -416,49 +570,52 @@
             pltpu.VMEM((SPAN, width), jnp.bfloat16),
             pltpu.VMEM((blocks, frames, 128), F32),
             pltpu.VMEM((8, frames), F32),
-            pltpu.VMEM((8, frames), F32),
-            pltpu.VMEM((total, frames // SPAN, frames, SPAN), jnp.bfloat16),
-            pltpu.SMEM((4, total), jnp.int32),
+            pltpu.VMEM((2, 8, 128), F32),
+            pltpu.VMEM((total - STARTED, frames // SPAN, frames, SPAN), jnp.bfloat16),
+            pltpu.SMEM((5, total), jnp.int32),
             pltpu.SemaphoreType.DMA((total,)),
-            pltpu.SemaphoreType.DMA((total,)),
+            pltpu.SemaphoreType.DMA((total - STARTED,)),
+            pltpu.SemaphoreType.DMA,
             pltpu.SemaphoreType.DMA,
         ],
         compiler_params=pltpu.CompilerParams(vmem_limit_bytes=60 * 1024 * 1024),
         name="first_pass",
-    )(*tables, student, every)
-
-
-def second_kernel(tiles, n_tm, dp_ref, slot_ref, valid_ref, ok_ref, s_ref, every, e_hbm, row_ref, far_ref, own_ref, out_ref,
+    )(*tables, student, every, sofar, cols)
+
+
+def second_kernel(tiles, n_tm, dp_ref, slot_ref, valid_ref, order_ref, ok_ref, s_ref, every, e_first, e_then, row_ref, far_ref, own_ref, out_ref,
                   s_buf, row_buf, w_buf, acc, e_buf, meta, sems, e_sems, row_sem, s_sem):
     me, tm = lax.axis_index("dp"), lax.axis_index("tm")
     frames, width = s_ref.shape[1], s_ref.shape[2]
     total = 2 * tiles
     spans_most = frames // SPAN
     scale = 1.0 / math.sqrt(width)
-    lay_table(meta, tiles, me, tm, n_tm, dp_ref, slot_ref, valid_ref)
+    lay_table(meta, tiles, me, tm, n_tm, dp_ref, slot_ref, valid_ref, order_ref)
 
     def fetch(e):
         return pltpu.make_async_copy(every.at[meta[0, e]], w_buf.at[e, :, pl.ds(0, width)], sems.at[e])
 
-    def load(e, carry):
-        fetch(e).start()
-
-        @pl.when(ok_ref[0] != 0)
-        def _():
-            by_shape(meta[1, e], meta[3, e // tiles], spans_most,
-                     lambda v, m: stash(e, v, m, e_buf, e_hbm, e_sems, False).start())
-        return carry
-    lax.fori_loop(0, total, load, 0)
+    def loader(store, skip):
+        def load(e, carry):
+            fetch(e).start()
+
+            @pl.when(ok_ref[0] != 0)
+            def _():
+                by_shape(meta[1, e], meta[4, e], spans_most,
+                         lambda v, m: stash(e, v, m, e_buf, store, e_sems, False, skip).start())
+            return carry
+        return load
+    lax.fori_loop(0, STARTED, loader(e_first, 0), 0)
+    lax.fori_loop(STARTED, total, loader(e_then, STARTED), 0)
     rows_in = pltpu.make_async_copy(row_ref, row_buf, row_sem)
     rows_in.start()
     acc[...] = jnp.zeros_like(acc)
 
     def lse_row(e, r):
-        a, k = e // tiles, e % tiles
-        return jnp.where(k == 0, own_ref[a, r:r + 1, :], far_ref[meta[2, e], r:r + 1, :])
+        return jnp.where(e < 2, own_ref[meta[3, e], r:r + 1, :], far_ref[meta[2, e], r:r + 1, :])
 
     def tile(e, carry):
-        a = e // tiles
+        a = meta[3, e]
         fetch(e).wait()
 
         def run(v, m):
@@ -467,10 +624,10 @@
                 rows = slice(r * 128, (r + 1) * 128)
                 weight = jnp.broadcast_to((0.5 * scale) * jnp.exp(-lse_row(e, r)), (128, 128)).T
                 w_buf[e, rows, width:] = (weight * w_buf[e, rows, :width].astype(F32)).astype(w_buf.dtype)
-            stash(e, v, m, e_buf, e_hbm, e_sems, False).wait()
+            stash(e, v, m, e_buf, e_first, e_sems, False, e).wait()
             lhs = jnp.concatenate([e_buf[e, j, :n, :] for j in range(v)], axis=1)
             acc[a, :n, :] += jnp.dot(lhs, w_buf[e, :v * SPAN, :], preferred_element_type=F32)
-        by_shape(meta[1, e], meta[3, a], spans_most, run)
+        by_shape(meta[1, e], meta[4, e], spans_most, run)
         return carry
 
     @pl.when(ok_ref[0] != 0)
@@ -485,7 +642,7 @@
         students.wait()
 
         def slow_tile(e, carry):
-            a = e // tiles
+            a = meta[3, e]
             fetch(e).wait()
 
             def slow_chunk(i, c):
@@ -500,7 +657,7 @@
                     part = part + scale * jnp.dot(g.astype(jnp.bfloat16), t, preferred_element_type=F32)
                 acc[a, rows, width:] = part
                 return c
-            lax.fori_loop(0, ceil_of(meta[3, a], half), slow_chunk, 0)
+            lax.fori_loop(0, ceil_of(meta[4, e], half), slow_chunk, 0)
             return carry
         lax.fori_loop(0, total, slow_tile, 0)
         acc[:, :, :width] = jnp.zeros_like(acc[:, :, :width])
@@ -508,18 +665,18 @@
     rows_in.wait()
     row = lax.broadcasted_iota(jnp.int32, (frames, width), 0)
     for a in range(2):
-        grad = row_buf[a] * acc[a, :, :width] + acc[a, :, width:] - scale * w_buf[a * tiles, :, :width].astype(F32)
-        out_ref[a] = jnp.where(row < meta[3, a], grad, 0.0).astype(out_ref.dtype)
-
-
-def second_pass(tables, ok, student, every, kept, rows, far, own, n_tm, tiles):
+        grad = row_buf[a] * acc[a, :, :width] + acc[a, :, width:] - scale * w_buf[a, :, :width].astype(F32)
+        out_ref[a] = jnp.where(row < meta[4, a], grad, 0.0).astype(out_ref.dtype)
+
+
+def second_pass(tables, ok, student, every, begun, kept, rows, far, own, n_tm, tiles):
     blocks, frames, width = student.shape
     total = blocks * tiles
     smem, vmem, hbm = (pl.BlockSpec(memory_space=m) for m in (pltpu.SMEM, pltpu.VMEM, pl.ANY))
     return pl.pallas_call(
         functools.partial(second_kernel, tiles, n_tm),
         out_shape=jax.ShapeDtypeStruct(student.shape, student.dtype),
-        in_specs=[smem, smem, smem, smem, hbm, hbm, hbm, hbm, vmem, vmem],
+        in_specs=[smem, smem, smem, smem, smem, hbm, hbm, hbm, hbm, hbm, vmem, vmem],
         out_specs=vmem,
         scratch_shapes=[
             pltpu.VMEM((blocks, frames, width), jnp.bfloat16),
@@ -527,7 +684,7 @@
             pltpu.VMEM((total, frames, 2 * width), jnp.bfloat16),
             pltpu.VMEM((blocks, frames, 2 * width), F32),
             pltpu.VMEM((total, frames // SPAN, frames, SPAN), jnp.bfloat16),
-            pltpu.SMEM((4, total), jnp.int32),
+            pltpu.SMEM((5, total), jnp.int32),
             pltpu.SemaphoreType.DMA((total,)),
             pltpu.SemaphoreType.DMA((total,)),
             pltpu.SemaphoreType.DMA,
@@ -535,7 +692,7 @@
         ],
         compiler_params=pltpu.CompilerParams(vmem_limit_bytes=60 * 1024 * 1024),
         name="second_pass",
-    )(*tables, ok, student, every, kept, rows, far, own)
+    )(*tables, ok, student, every, begun, kept, rows, far, own)
 
 
 def exchange_kernel(n_dp, n_tm, valid_ref, ask_ref, side_ref, send_ref, own_ref, sum_ref, far_ref, lse_ref, loss_ref,
@@ -624,11 +781,12 @@
     blocks, frames, width = student.shape
     tiles = partner_dp.shape[1] + 1
     tables = (partner_dp.T, partner_slot.T, valid_frames)
-    every, ask, side = gather(teacher, student, tables, n_dp, n_tm)
+    every, begun, sofar, ask, side, order, cols = gather(teacher, student, tables, n_dp, n_tm)
     every = every.reshape(n_dp * blocks, frames, width)
-    rows, send, own, ok, sums, kept = first_pass(tables, student, every, n_dp, n_tm, tiles)
+    tables = tables + (order,)
+    rows, send, own, ok, sums, kept = first_pass(tables, student, every, sofar, cols, n_dp, n_tm, tiles)
     far, lse, loss = exchange(valid_frames, ask, side, send, own, sums, n_tm)
-    grad = second_pass(tables, ok, student, every, kept, rows, far, lse, n_tm, tiles)
+    grad = second_pass(tables, ok, student, every, begun, kept, rows, far, lse, n_tm, tiles)
     return (loss[0], grad)
 
 

time: 491 us -> 486 us (0.990)
  Pallas kernels: 489 us -> 483 us
    pallas_call x1, Pallas kernels: 195 us -> 186 us  [first_pass(): pl.pallas_call(functools.partial(first_kernel, tiles, n_tm), out_shape=(j...]
where the time goes in v4:
time: 486 us
  Pallas kernels  483 us (99%)
    pallas_call x1, Pallas kernels, second_pass(): pl.pallas_call(functools.partial(second_kernel, tiles, n_tm), out_shape=j...  222 us
    pallas_call x1, Pallas kernels, first_pass(): pl.pallas_call(functools.partial(first_kernel, tiles, n_tm), out_shape=(j...  186 us
    pallas_call x1, Pallas kernels, gather(): pl.pallas_call(functools.partial(gather_kernel, n_tm), out_shape=(jax.Sha...  55.3 us
    pallas_call x1, Pallas kernels, exchange(): pl.pallas_call(functools.partial(exchange_kernel, n_dp, n_tm), out_shape=...  19.7 us

profile of v4, /device:TPU:18, one launch (start us, length us, event | category | flops | bytes accessed | tf_op | source)
XLA Modules:
  0.0 485.8 jit_solution(7654748676214937312)
XLA Ops:
  0.6 55.3 %gather.1 = (bf16[32,2,1024,128]{3,2,1,0:T(8,128)(2,1)}, bf16[12,4,1024,256]{3,2,1,0:T(8,128)(2,1)}, f32[2,1024,128]{2,1,0:T(8,128)}, f32[32,3,8,128]{3,2,1,0:T(...) custom-call(bf16[2,1024,128]{2,1,0:T(8,128)(2,1)} %t_ref.1, bf16[2,1024,128]{2,1,0:T(8,128)(2,1)} %s_ref.5, ...), custom_call_target="tpu_custom_call" | custom-call | tf_op jit(solution)/shard_map/gather/pallas_call | solution.py:321
  56.0 186.0 %first_pass.1 = (f32[2,1024,128]{2,1,0:T(8,128)}, f32[32,8,128]{2,1,0:T(8,128)}, f32[2,8,128]{2,1,0:T(8,128)}, s32[1]{0:T(128)}, f32[8,128]{1,0:T(8,128)}, /*index=5*/bf16[6,4,1024,256]{3,2,1,0:T(8,128)(2,1)}) custom-call(s32[8,256]{1,0:T(8,128)} %bitcast.8, s32[8,256]{1,0:T(8,128)} %bitcast.12, s32[256]{0:T(256)} %valid_ref.7, ...), custom_call_target="tpu_custom_call" | custom-call | tf_op jit(solution)/shard_map/first_pass/pallas_call | solution.py:552
  241.9 19.7 %exchange.1 = (f32[32,8,128]{2,1,0:T(8,128)}, f32[2,8,128]{2,1,0:T(8,128)}, f32[1]{0:T(128)}) custom-call(s32[256]{0:T(256)} %valid_ref.7, f32[32,3,8,128]{3,2,1,0:T(8,128)} %get-tuple-element.18.ask_ref, f32[2,8,128]{2,1,0:T(8,128)} %get-tuple-element.19.side_ref, f32[32,8,128]{2,1,0:T(8,128)} %get-tuple-element.24.send_ref, ...), custom_call_target="tpu_custom_call" | custom-call | tf_op jit(solution)/shard_map/exchange/pallas_call | solution.py:761
  261.7 222.4 %second_pass.1 = bf16[2,1024,128]{2,1,0:T(8,128)(2,1)} custom-call(s32[8,256]{1,0:T(8,128)} %bitcast.9, s32[8,256]{1,0:T(8,128)} %bitcast.13, s32[256]{0:T(256)} %valid_ref.7, s32[16]{0:T(128)} %get-tuple-element.20.order_ref, s32[1]{0:T(128)} %get-tuple-element.28.ok_ref, bf16[2,1024,128]{2,1,0:T(8,128)(2,1)} %s_ref.5, bf16[64,1024,128]{2,1,0:T(8,128)(2,1)} %bitcast.5, ...), custom_call_target="tpu_custom_call" | custom-call | tf_op jit(solution)/shard_map/second_pass/pallas_call | solution.py:676

commit v5 on v4

--- a/solution.py
+++ b/solution.py
@@ -390,12 +390,12 @@
     return pltpu.make_async_copy(near, far, sems.at[e]) if out else pltpu.make_async_copy(far, near, sems.at[e])
 
 
-def by_shape(keys, count, most, run):
-    spans, units = ceil_of(keys, SPAN), ceil_of(count, UNIT)
+def by_shape(keys, count, most, run, least=1):
+    spans, units = ceil_of(keys, SPAN), jnp.maximum(ceil_of(count, UNIT), least)
     for v in range(1, most + 1):
         @pl.when(spans == v)
         def _():
-            for m in range(1, most + 1):
+            for m in range(least, most + 1):
                 pl.when(units == m)(functools.partial(run, v, m))
 
 
@@ -584,7 +584,7 @@
 
 
 def second_kernel(tiles, n_tm, dp_ref, slot_ref, valid_ref, order_ref, ok_ref, s_ref, every, e_first, e_then, row_ref, far_ref, own_ref, out_ref,
-                  s_buf, row_buf, w_buf, acc, e_buf, meta, sems, e_sems, row_sem, s_sem):
+                  s_buf, row_buf, t_buf, w_even, w_odd, acc, e_buf, meta, sems, e_sems, row_sem, s_sem):
     me, tm = lax.axis_index("dp"), lax.axis_index("tm")
     frames, width = s_ref.shape[1], s_ref.shape[2]
     total = 2 * tiles
@@ -593,7 +593,7 @@
     lay_table(meta, tiles, me, tm, n_tm, dp_ref, slot_ref, valid_ref, order_ref)
 
     def fetch(e):
-        return pltpu.make_async_copy(every.at[meta[0, e]], w_buf.at[e, :, pl.ds(0, width)], sems.at[e])
+        return pltpu.make_async_copy(every.at[meta[0, e]], t_buf.at[e], sems.at[e])
 
     def loader(store, skip):
         def load(e, carry):
@@ -602,7 +602,7 @@
             @pl.when(ok_ref[0] != 0)
             def _():
                 by_shape(meta[1, e], meta[4, e], spans_most,
-                         lambda v, m: stash(e, v, m, e_buf, store, e_sems, False, skip).start())
+                         lambda v, m: stash(e, v, m, e_buf, store, e_sems, False, skip).start(), 2)
             return carry
         return load
     lax.fori_loop(0, STARTED, loader(e_first, 0), 0)
@@ -614,25 +614,36 @@
     def lse_row(e, r):
         return jnp.where(e < 2, own_ref[meta[3, e], r:r + 1, :], far_ref[meta[2, e], r:r + 1, :])
 
-    def tile(e, carry):
+    def weigh(e, w_buf):
+        for r in range(frames // 128):
+            rows = slice(r * 128, (r + 1) * 128)
+            weight = jnp.broadcast_to((0.5 * scale) * jnp.exp(-lse_row(e, r)), (128, 128)).T
+            w_buf[rows, :] = (weight * t_buf[e, rows, :].astype(F32)).astype(w_buf.dtype)
+
+    def tile(e, w_buf, w_next):
         a = meta[3, e]
-        fetch(e).wait()
+        then = jnp.minimum(e + 1, total - 1)
+        pl.when(e + 1 < total)(lambda: fetch(then).wait())
 
         def run(v, m):
             n = UNIT * m
-            for r in range(v * SPAN // 128):
-                rows = slice(r * 128, (r + 1) * 128)
-                weight = jnp.broadcast_to((0.5 * scale) * jnp.exp(-lse_row(e, r)), (128, 128)).T
-                w_buf[e, rows, width:] = (weight * w_buf[e, rows, :width].astype(F32)).astype(w_buf.dtype)
             stash(e, v, m, e_buf, e_first, e_sems, False, e).wait()
             lhs = jnp.concatenate([e_buf[e, j, :n, :] for j in range(v)], axis=1)
-            acc[a, :n, :] += jnp.dot(lhs, w_buf[e, :v * SPAN, :], preferred_element_type=F32)
-        by_shape(meta[1, e], meta[4, e], spans_most, run)
-        return carry
+            rhs = jnp.concatenate([t_buf[e, :v * SPAN, :], w_buf[:v * SPAN, :]], axis=1)
+            acc[a, :n, :] += jnp.dot(lhs, rhs, preferred_element_type=F32)
+            weigh(then, w_next)
+        by_shape(meta[1, e], meta[4, e], spans_most, run, 2)
 
     @pl.when(ok_ref[0] != 0)
     def _():
-        lax.fori_loop(0, total, tile, 0)
+        fetch(0).wait()
+        weigh(0, w_even)
+
+        def pair(i, carry):
+            tile(2 * i, w_even, w_odd)
+            tile(2 * i + 1, w_odd, w_even)
+            return carry
+        lax.fori_loop(0, total // 2, pair, 0)
 
     @pl.when(ok_ref[0] == 0)
     def _():
@@ -649,7 +660,7 @@
                 rows = pl.ds(pl.multiple_of(i * half, half), half)
                 part = acc[a, rows, width:]
                 for j in range(frames // half):
-                    t = w_buf[e, j * half:(j + 1) * half, :width]
+                    t = t_buf[e, j * half:(j + 1) * half, :]
                     inside = lax.broadcasted_iota(jnp.int32, (half, half), 1) + j * half < meta[1, e]
                     sc = nt(s_buf[a, rows, :], t) * scale
                     g = 0.5 * (jnp.exp(jnp.where(inside, sc - row_buf[a, rows, :], -BIG))
@@ -665,7 +676,7 @@
     rows_in.wait()
     row = lax.broadcasted_iota(jnp.int32, (frames, width), 0)
     for a in range(2):
-        grad = row_buf[a] * acc[a, :, :width] + acc[a, :, width:] - scale * w_buf[a, :, :width].astype(F32)
+        grad = row_buf[a] * acc[a, :, :width] + acc[a, :, width:] - scale * t_buf[a].astype(F32)
         out_ref[a] = jnp.where(row < meta[4, a], grad, 0.0).astype(out_ref.dtype)
 
 
@@ -681,7 +692,9 @@
         scratch_shapes=[
             pltpu.VMEM((blocks, frames, width), jnp.bfloat16),
             pltpu.VMEM((blocks, frames, 128), F32),
-            pltpu.VMEM((total, frames, 2 * width), jnp.bfloat16),
+            pltpu.VMEM((total, frames, width), jnp.bfloat16),
+            pltpu.VMEM((frames, width), jnp.bfloat16),
+            pltpu.VMEM((frames, width), jnp.bfloat16),
             pltpu.VMEM((blocks, frames, 2 * width), F32),
             pltpu.VMEM((total, frames // SPAN, frames, SPAN), jnp.bfloat16),
             pltpu.SMEM((5, total), jnp.int32),
@@ -696,8 +709,10 @@
 
 
 def exchange_kernel(n_dp, n_tm, valid_ref, ask_ref, side_ref, send_ref, own_ref, sum_ref, far_ref, lse_ref, loss_ref,
-                    inc, reply, across, column, s1, r1, s2, r2, s3, r3, s4, r4):
+                    inc, reply, across, ask_buf, s1, r1, s2, r2, s3, r3, ask_sem):
     me, tm = lax.axis_index("dp"), lax.axis_index("tm")
+    asks = pltpu.make_async_copy(ask_ref, ask_buf, ask_sem)
+    asks.start()
     others = [(me + o) % n_dp for o in range(1, n_dp)]
     beside = [(tm + o) % n_tm for o in range(1, n_tm)]
     barrier = pltpu.get_barrier_semaphore()
@@ -715,44 +730,43 @@
     for to in others:
         ship(send_ref.at[to], inc.at[me], s1, r1, (to, tm))
     settle(inc, r1, n_dp - 1)
+    asks.wait()
     terms = sum_ref[...] + side_ref[0]
     frame = lax.broadcasted_iota(jnp.int32, (8, 128), 0) * 128 + lax.broadcasted_iota(jnp.int32, (8, 128), 1)
     for a in range(2):
         best = own_ref[a]
         for p in range(n_dp):
-            best = jnp.maximum(best, inc[p] + ask_ref[p, a])
+            best = jnp.maximum(best, inc[p] + ask_buf[p, a])
         total = jnp.exp(own_ref[a] - best)
         for p in range(n_dp):
-            total = total + jnp.exp(inc[p] + ask_ref[p, a] - best)
+            total = total + jnp.exp(inc[p] + ask_buf[p, a] - best)
         lse = jnp.where(frame < valid_ref[(me * n_tm + tm) * 2 + a], best + jnp.log(total), 0.0)
         lse_ref[a] = lse
         terms = terms + lse
-    across[tm] = terms
+    terms = jnp.sum(terms, axis=0, keepdims=True)
     for p in range(n_dp):
-        share = ask_ref[p, 2]
-        reply[p] = lse_ref[0] * (1.0 - share) + lse_ref[1] * share
+        share = ask_buf[p, 2]
+        reply[p, :8, :] = lse_ref[0] * (1.0 - share) + lse_ref[1] * share
+        reply[p, 8:9, :] = terms
     far_ref[me] = reply[me]
+    sent = pl.ds(0, 9)
+    for to in others:
+        ship(reply.at[to, sent], far_ref.at[me, sent], s2, r2, (to, tm))
+    settle(far_ref.at[:, sent], r2, n_dp - 1)
+    rows = far_ref[0, 8:9, :]
+    for p in range(1, n_dp):
+        rows = rows + far_ref[p, 8:9, :]
+    across[tm] = jnp.broadcast_to(rows, (8, 128))
     for to in beside:
         ship(across.at[tm], across.at[tm], s3, r3, (me, to))
-    for to in others:
-        ship(reply.at[to], far_ref.at[me], s2, r2, (to, tm))
     settle(across, r3, n_tm - 1)
     rows = across[0]
     for t in range(1, n_tm):
         rows = rows + across[t]
-    column[me] = rows
-    for to in others:
-        ship(column.at[me], column.at[me], s4, r4, (to, tm))
-    settle(far_ref, r2, n_dp - 1)
-    settle(column, r4, n_dp - 1)
-    rows = column[0]
-    for p in range(1, n_dp):
-        rows = rows + column[p]
-    loss_ref[0] = jnp.sum(rows * side_ref[1])
+    loss_ref[0] = jnp.sum(rows[0:1] * side_ref[1, 0:1, :])
     settle(send_ref, s1, n_dp - 1)
-    settle(reply, s2, n_dp - 1)
+    settle(reply.at[:, sent], s2, n_dp - 1)
     settle(across, s3, n_tm - 1)
-    settle(column, s4, n_dp - 1)
 
 
 def exchange(valid, ask, side, send, own, sums, n_tm):
@@ -761,16 +775,16 @@
     return pl.pallas_call(
         functools.partial(exchange_kernel, n_dp, n_tm),
         out_shape=(
-            jax.ShapeDtypeStruct((n_dp, 8, 128), F32),
+            jax.ShapeDtypeStruct((n_dp, 16, 128), F32),
             jax.ShapeDtypeStruct((2, 8, 128), F32),
             jax.ShapeDtypeStruct((1,), F32),
         ),
-        in_specs=[smem] + [vmem] * 5,
+        in_specs=[smem, pl.BlockSpec(memory_space=pl.ANY)] + [vmem] * 4,
         out_specs=(vmem, vmem, smem),
         scratch_shapes=[
-            pltpu.VMEM((n_dp, 8, 128), F32), pltpu.VMEM((n_dp, 8, 128), F32),
-            pltpu.VMEM((n_tm, 8, 128), F32), pltpu.VMEM((n_dp, 8, 128), F32),
-        ] + [pltpu.SemaphoreType.DMA] * 8,
+            pltpu.VMEM((n_dp, 8, 128), F32), pltpu.VMEM((n_dp, 16, 128), F32),
+            pltpu.VMEM((n_tm, 8, 128), F32), pltpu.VMEM(ask.shape, F32),
+        ] + [pltpu.SemaphoreType.DMA] * 7,
         compiler_params=pltpu.CompilerParams(collective_id=1, has_side_effects=True),
         name="exchange",
     )(valid, ask, side, send, own, sums)

time: 486 us -> 486 us (level)
  no operation moved by 1% of the time
where the time goes in v5:
time: 486 us
  Pallas kernels  484 us (100%)
    pallas_call x1, Pallas kernels, second_pass(): pl.pallas_call(functools.partial(second_kernel, tiles, n_tm), out_shape=j...  222 us
    pallas_call x1, Pallas kernels, first_pass(): pl.pallas_call(functools.partial(first_kernel, tiles, n_tm), out_shape=(j...  186 us
    pallas_call x1, Pallas kernels, gather(): pl.pallas_call(functools.partial(gather_kernel, n_tm), out_shape=(jax.Sha...  55.3 us
    pallas_call x1, Pallas kernels, exchange(): pl.pallas_call(functools.partial(exchange_kernel, n_dp, n_tm), out_shape=...  19.9 us

profile of v5, /device:TPU:18, one launch (start us, length us, event | category | flops | bytes accessed | tf_op | source)
XLA Modules:
  0.0 486.0 jit_solution(1321885525629320277)
XLA Ops:
  0.6 55.3 %gather.1 = (bf16[32,2,1024,128]{3,2,1,0:T(8,128)(2,1)}, bf16[12,4,1024,256]{3,2,1,0:T(8,128)(2,1)}, f32[2,1024,128]{2,1,0:T(8,128)}, f32[32,3,8,128]{3,2,1,0:T(...) custom-call(bf16[2,1024,128]{2,1,0:T(8,128)(2,1)} %t_ref.1, bf16[2,1024,128]{2,1,0:T(8,128)(2,1)} %s_ref.5, ...), custom_call_target="tpu_custom_call" | custom-call | tf_op jit(solution)/shard_map/gather/pallas_call | solution.py:321
  56.0 186.0 %first_pass.1 = (f32[2,1024,128]{2,1,0:T(8,128)}, f32[32,8,128]{2,1,0:T(8,128)}, f32[2,8,128]{2,1,0:T(8,128)}, s32[1]{0:T(128)}, f32[8,128]{1,0:T(8,128)}, /*index=5*/bf16[6,4,1024,256]{3,2,1,0:T(8,128)(2,1)}) custom-call(s32[8,256]{1,0:T(8,128)} %bitcast.8, s32[8,256]{1,0:T(8,128)} %bitcast.12, s32[256]{0:T(256)} %valid_ref.7, ...), custom_call_target="tpu_custom_call" | custom-call | tf_op jit(solution)/shard_map/first_pass/pallas_call | solution.py:552
  241.9 19.9 %exchange.1 = (f32[32,16,128]{2,1,0:T(8,128)}, f32[2,8,128]{2,1,0:T(8,128)}, f32[1]{0:T(128)}) custom-call(s32[256]{0:T(256)} %valid_ref.7, f32[32,3,8,128]{3,2,1,0:T(8,128)} %get-tuple-element.18.ask_ref, f32[2,8,128]{2,1,0:T(8,128)} %get-tuple-element.19.side_ref, f32[32,8,128]{2,1,0:T(8,128)} %get-tuple-element.24.send_ref, ...), custom_call_target="tpu_custom_call" | custom-call | tf_op jit(solution)/shard_map/exchange/pallas_call | solution.py:775
  261.9 222.3 %second_pass.1 = bf16[2,1024,128]{2,1,0:T(8,128)(2,1)} custom-call(s32[8,256]{1,0:T(8,128)} %bitcast.9, s32[8,256]{1,0:T(8,128)} %bitcast.13, s32[256]{0:T(256)} %valid_ref.7, s32[16]{0:T(128)} %get-tuple-element.20.order_ref, s32[1]{0:T(128)} %get-tuple-element.28.ok_ref, bf16[2,1024,128]{2,1,0:T(8,128)(2,1)} %s_ref.5, bf16[64,1024,128]{2,1,0:T(8,128)(2,1)} %bitcast.5, ...), custom_call_target="tpu_custom_call" | custom-call | tf_op jit(solution)/shard_map/second_pass/pallas_call | solution.py:687
